TPU v7x, 256 devices: a whole 4x4x8 slice. The times are simulated.
256 devices in a mesh: gx: 8 (over z_hi, y), gy: 4 (over z_lo), gz: 8 (over x, core).
Axes of the slice: x: 4, y: 4, z: 8 (z_hi: 2, z_lo: 4; z = z_hi * 4 + z_lo), core: 2. Of those that a mesh axis runs over, the one named last changes fastest.
Arguments:
- displacement: float32 [3, 32, 128, 2048], P(None, 'gx', 'gy', 'gz'), may hold values from -13 to 13
- density: float32 [32, 128, 2048], P('gx', 'gy', 'gz'), may hold values from 0.05 to 1
- material: int32 [32, 128, 2048], P('gx', 'gy', 'gz'), may hold values from 0 to 2
- fixed_mask: int32 [32, 128, 2048], P('gx', 'gy', 'gz'), may hold values 0 or 1
Outputs:
- adjoint: float32 [3, 32, 128, 2048], P(None, 'gx', 'gy', 'gz')
- sensitivity: float32 [32, 128, 2048], P('gx', 'gy', 'gz')
All inputs are finite; a program needn't handle non-finite values. No bound on the sum of `fixed_mask` on one device may be relied on, other than what follows from the above.
Results may differ from a plain program's by a relative error of at most 0.000033.
Values sent between devices are 32-bit elements; how exact they have to be, the bound alone decides.
A program may use at most 64 MiB of HBM per device.

v0:
```python
import jax
import jax.numpy as jnp
from jax import lax
from jax.sharding import PartitionSpec as P

lame_first = 0.577
lame_shear = 0.385
relax_weight = 0.6
tiny_shift = 1e-06
diag_scale = (0.577 + 4.0 * 0.385) / 16.0


def padded(block, sides, width):
    for axis, dim in sides:
        count = lax.axis_size(axis)
        forward = [(i, i + 1) for i in range(count - 1)]
        backward = [(target, source) for source, target in forward]
        low = lax.ppermute(
            lax.slice_in_dim(block, block.shape[dim] - width, None, axis=dim), axis, forward
        )
        high = lax.ppermute(lax.slice_in_dim(block, 0, width, axis=dim), axis, backward)
        block = jnp.concatenate([low, block, high], axis=dim)
    return block


def pair_sum(values, which_axis):
    length = values.shape[which_axis]
    return lax.slice_in_dim(values, 1, length, axis=which_axis) + lax.slice_in_dim(
        values, 0, length - 1, axis=which_axis
    )


def differ(values, which_axis):
    length = values.shape[which_axis]
    return lax.slice_in_dim(values, 1, length, axis=which_axis) - lax.slice_in_dim(
        values, 0, length - 1, axis=which_axis
    )


def along_x(values):
    return 0.25 * pair_sum(pair_sum(differ(values, -3), -2), -1)


def along_y(values):
    return 0.25 * pair_sum(pair_sum(differ(values, -2), -3), -1)


def along_z(values):
    return 0.25 * pair_sum(pair_sum(differ(values, -1), -3), -2)


def strains(nodal_field):
    grad_x = along_x(nodal_field)
    grad_y = along_y(nodal_field)
    grad_z = along_z(nodal_field)
    return jnp.stack(
        [
            grad_x[0],
            grad_y[1],
            grad_z[2],
            grad_y[0] + grad_x[1],
            grad_z[1] + grad_y[2],
            grad_x[2] + grad_z[0],
        ]
    )


def stiffen(vector):
    trace_sum = vector[0] + vector[1] + vector[2]
    return jnp.stack(
        [
            lame_first * trace_sum + 2.0 * lame_shear * vector[0],
            lame_first * trace_sum + 2.0 * lame_shear * vector[1],
            lame_first * trace_sum + 2.0 * lame_shear * vector[2],
            lame_shear * vector[3],
            lame_shear * vector[4],
            lame_shear * vector[5],
        ]
    )


def mises_quad(stress):
    return (
        stress[0] ** 2
        + stress[1] ** 2
        + stress[2] ** 2
        - stress[0] * stress[1]
        - stress[1] * stress[2]
        - stress[2] * stress[0]
        + 3.0 * (stress[3] ** 2 + stress[4] ** 2 + stress[5] ** 2)
    )


def mises_slope(stress):
    return jnp.stack(
        [
            2.0 * stress[0] - stress[1] - stress[2],
            2.0 * stress[1] - stress[0] - stress[2],
            2.0 * stress[2] - stress[0] - stress[1],
            6.0 * stress[3],
            6.0 * stress[4],
            6.0 * stress[5],
        ]
    )


def forces(dual_stress):
    part_x = along_x(jnp.stack([dual_stress[0], dual_stress[3], dual_stress[5]]))
    part_y = along_y(jnp.stack([dual_stress[3], dual_stress[1], dual_stress[4]]))
    part_z = along_z(jnp.stack([dual_stress[5], dual_stress[4], dual_stress[2]]))
    return -(part_x + part_y + part_z)


def node_weight(stiffness):
    return diag_scale * pair_sum(pair_sum(pair_sum(stiffness, -3), -2), -1)


def factors(density, material):
    design = material == 1
    solid = material == 2
    root = jnp.sqrt(density)
    stiffness = 0.001 + jnp.where(design, density**3, jnp.where(solid, 1.0, 0.0))
    stress_factor = jnp.where(design, root, jnp.where(solid, 1.0, 0.0))
    stiff_slope = jnp.where(design, 3.0 * density**2, 0.0)
    stress_slope = jnp.where(design, 0.5 / root, 0.0)
    return (stiffness, stress_factor, stiff_slope, stress_slope)


def ghost_thin(values):
    return padded(values, (("gx", 1), ("gy", 2), ("gz", 3)), 1)


def owned_part(values, offset, local_shape):
    return values[
        ...,
        offset : offset + local_shape[0],
        offset : offset + local_shape[1],
        offset : offset + local_shape[2],
    ]


def per_device(displacement, density, material, fixed_mask):
    local_shape = density.shape
    stiffness, stress_factor, stiff_slope, stress_slope = factors(density, material)
    free_nodes = 1.0 - fixed_mask.astype(jnp.float32)
    offset = 1
    packed = ghost_thin(jnp.concatenate([displacement, stiffness[None], stress_factor[None]], 0))
    elem_stiff = packed[3, :-1, :-1, :-1]
    elem_stress = packed[4, :-1, :-1, :-1]
    unit_stress = stiffen(strains(packed[:3]))
    unit_mises = mises_quad(unit_stress)
    mises_square = elem_stress**2 * unit_mises
    partial_value = jnp.sum(owned_part(mises_square, offset, local_shape) ** 4)
    global_sum = lax.psum(partial_value, ("gx", "gy", "gz"))
    element_count = (
        local_shape[0]
        * local_shape[1]
        * local_shape[2]
        * lax.axis_size("gx")
        * lax.axis_size("gy")
        * lax.axis_size("gz")
    )
    factor = (global_sum / element_count + tiny_shift) ** (-0.875)
    weight = factor * mises_square**3
    dual_stress = stiffen(0.5 * weight * elem_stress**2 * mises_slope(unit_stress))
    load_field = forces(dual_stress)
    diagonal = node_weight(elem_stiff) + (1.0 - free_nodes)
    first_sweep = free_nodes * load_field / diagonal
    applied = forces(elem_stiff * stiffen(strains(ghost_thin(first_sweep))))
    adjoint = first_sweep + relax_weight * free_nodes * (load_field - applied) / diagonal
    second_ext = ghost_thin(adjoint)[:, 1:, 1:, 1:]
    strain_adj = strains(second_ext)
    unit_owned = owned_part(unit_stress, offset, local_shape)
    sensitivity = owned_part(weight, offset, local_shape) * stress_factor * owned_part(
        unit_mises, offset, local_shape
    ) * stress_slope - stiff_slope * jnp.sum(strain_adj * unit_owned, axis=0)
    return (adjoint, sensitivity)


def solution(mesh):
    placed = (
        P(None, "gx", "gy", "gz"),
        P("gx", "gy", "gz"),
        P("gx", "gy", "gz"),
        P("gx", "gy", "gz"),
    )
    return jax.shard_map(
        per_device,
        mesh=mesh,
        in_specs=placed,
        out_specs=(P(None, "gx", "gy", "gz"), P("gx", "gy", "gz")),
        check_vma=False,
    )
```

profile of v0, /device:TPU:89, one launch (start us, length us, event | category | flops | bytes accessed | tf_op | source)
XLA Modules:
  0.0 243.2 jit_solution(15795247586208192462)
XLA Ops:
  0.6 1.1 fusion.41
  1.7 1.0 fusion.55
  2.7 1.0 pad_maximum_fusion.23
  3.7 6.7 %collective-permute-start = (f32[5,1,32,256]{3,2,1,0:T(8,128)S(1)}, f32[5,1,32,256]{3,2,1,0:T(8,128)S(1)}, u32[]{:S(2)}, u32[]{:S(2)}) collective-permute-start(f32[5,1,32,256]{3,2,1,0:T(8,128)S(1)} %get-tuple-element.48), channel_id=1, source_target_pairs={{0,32},{32,64},{64,96},{96,128},{128,160},{160,192},{192,224},{1,3... | collective-permute-start | bytes 491528 | tf_op jit(solution)/shard_map/ppermute | solution.py:18
  10.4 1.9 collective-permute-start.1
  12.3 4.6 %collective-permute-done = f32[5,1,32,256]{3,2,1,0:T(8,128)S(1)} collective-permute-done((f32[5,1,32,256]{3,2,1,0:T(8,128)S(1)}, f32[5,1,32,256]{3,2,1,0:T(8,128)S(1)}, u32[]{:S(2)}, u32[]{:S(2)}) %collective-permute-start) | collective-permute-done | bytes 163872 | tf_op jit(solution)/shard_map/ppermute | solution.py:18
  16.9 10.1 %collective-permute-done.1 = f32[5,1,32,256]{3,2,1,0:T(8,128)S(1)} collective-permute-done((f32[5,1,32,256]{3,2,1,0:T(8,128)S(1)}, f32[5,1,32,256]{3,2,1,0:T(8,128)S(1)}, u32[]{:S(2)}, u32[]{:S(2)}) %collective-permute-start.1) | collective-permute-done | bytes 163872 | tf_op jit(solution)/shard_map/ppermute | solution.py:21
  27.1 1.9 collective-permute-start.2
  29.1 3.4 %collective-permute-start.3 = (f32[5,6,1,256]{3,1,2,0:T(8,128)S(1)}, f32[5,6,1,256]{3,1,2,0:T(8,128)S(1)}, u32[]{:S(2)}, u32[]{:S(2)}) collective-permute-start(f32[5,6,1,256]{3,1,2,0:T(8,128)S(1)} %copy.58), channel_id=1, source_target_pairs={{8,0},{16,8},{24,16},{9,1},{17,9},{25,17},{10,2},{18,10},{26,18},{... | collective-permute-start | bytes 92168 | tf_op jit(solution)/shard_map/ppermute | solution.py:21
  32.5 3.2 %copy.39 = f32[5,6,32,256]{2,1,3,0:T(8,128)} copy(f32[5,6,32,256]{3,2,1,0:T(8,128)S(1)} %pad_maximum_fusion.5) | data formatting | bytes 1966080 | tf_op jit(solution)/shard_map/concatenate | solution.py:22
  35.6 3.1 %copy.38 = f32[5,6,1,256]{2,1,3,0:T(8,128)} copy(f32[5,6,1,256]{3,1,2,0:T(8,128)S(1)} %collective-permute-done.2) | data formatting | bytes 61440 | tf_op jit(solution)/shard_map/ppermute | solution.py:18
  38.7 3.1 %copy.40 = f32[5,6,1,256]{2,1,3,0:T(8,128)} copy(f32[5,6,1,256]{3,1,2,0:T(8,128)S(1)} %collective-permute-done.3) | data formatting | bytes 61440 | tf_op jit(solution)/shard_map/ppermute | solution.py:21
  41.8 8.3 %pad_maximum_fusion = f32[5,6,34,256]{2,1,3,0:T(8,128)S(1)} fusion(f32[5,6,1,256]{2,1,3,0:T(8,128)} %copy.40, f32[5,6,32,256]{2,1,3,0:T(8,128)} %copy.39, f32[5,6,1,256]{2,1,3,0:T(8,128)} %copy.38), kind=kLoop, calls=%fused_computation | loop fusion | flops 522240 | bytes 2088960 | tf_op jit(solution)/shard_map/concatenate | solution.py:22
  50.2 2.3 copy-done
  52.5 4.9 %collective-permute-start.4 = (f32[5,6,34,1]{2,1,3,0:T(8,128)S(1)}, f32[5,6,34,1]{2,1,3,0:T(8,128)S(1)}, u32[]{:S(2)}, u32[]{:S(2)}) collective-permute-start(f32[5,6,34,1]{2,1,3,0:T(8,128)S(1)} %get-tuple-element.24), channel_id=1, source_target_pairs={{0,1},{1,2},{2,3},{3,4},{4,5},{5,6},{6,7},{8,9},{9,10},{10,11},{11... | collective-permute-start | bytes 12248 | tf_op jit(solution)/shard_map/ppermute | solution.py:18
  57.4 4.1 %copy.42 = f32[5,6,34,256]{3,2,1,0:T(8,128)S(1)} copy(f32[5,6,34,256]{2,1,3,0:T(8,128)} %copy-done) | data formatting | bytes 2088960 | tf_op jit(solution)/shard_map/concatenate | solution.py:22
  61.6 1.9 collective-permute-start.5
  63.8 0.9 fusion.38
  64.7 1.9 collective-permute-done.5
  70.2 1.2 bitcast_multiply_fusion
  71.4 0.8 subtract_dynamic-update-slice_fusion.2
  73.6 72.1 %psum.7 = f32[]{:T(128)} all-reduce(f32[]{:T(128)} %fusion.45), channel_id=1, replica_groups=mesh['gx'=8,'gy'=4,'gz'=8] {'gx','gy','gz'}, use_global_device_ids=true, to_apply=%region_1.2 | all-reduce | flops 1 | bytes 8 | tf_op jit(solution)/shard_map/psum | solution.py:154
  145.7 1.8 subtract_dynamic-update-slice_fusion.1
  147.5 1.8 subtract_dynamic-update-slice_fusion
  150.0 2.0 multiply_dynamic-update-slice_fusion.5
  152.0 1.9 multiply_dynamic-update-slice_fusion.4
  153.9 1.9 multiply_dynamic-update-slice_fusion.3
  155.9 1.6 broadcast_multiply_fusion.1
  159.8 5.1 %collective-permute-start.6 = (f32[3,1,32,256]{3,2,1,0:T(8,128)S(1)}, f32[3,1,32,256]{3,2,1,0:T(8,128)S(1)}, u32[]{:S(2)}, u32[]{:S(2)}) collective-permute-start(f32[3,1,32,256]{3,2,1,0:T(8,128)S(1)} %get-tuple-element.56), channel_id=1, source_target_pairs={{0,32},{32,64},{64,96},{96,128},{128,160},{160,192},{192,224},{1,3... | collective-permute-start | bytes 294920 | tf_op jit(solution)/shard_map/ppermute | solution.py:18
  164.9 1.9 collective-permute-start.7
  166.9 9.4 %collective-permute-done.7 = f32[3,1,32,256]{3,2,1,0:T(8,128)S(1)} collective-permute-done((f32[3,1,32,256]{3,2,1,0:T(8,128)S(1)}, f32[3,1,32,256]{3,2,1,0:T(8,128)S(1)}, u32[]{:S(2)}, u32[]{:S(2)}) %collective-permute-start.7) | collective-permute-done | bytes 98336 | tf_op jit(solution)/shard_map/ppermute | solution.py:21
  176.3 7.6 %collective-permute-start.9 = (f32[3,6,1,256]{3,1,2,0:T(8,128)S(1)}, f32[3,6,1,256]{3,1,2,0:T(8,128)S(1)}, u32[]{:S(2)}, u32[]{:S(2)}) collective-permute-start(f32[3,6,1,256]{3,1,2,0:T(8,128)S(1)} %copy.60), channel_id=1, source_target_pairs={{8,0},{16,8},{24,16},{9,1},{17,9},{25,17},{10,2},{18,10},{26,18},{... | collective-permute-start | bytes 55304 | tf_op jit(solution)/shard_map/ppermute | solution.py:21
  184.0 1.9 collective-permute-start.8
  186.0 2.6 %collective-permute-done.8 = f32[3,6,1,256]{3,1,2,0:T(8,128)S(1)} collective-permute-done((f32[3,6,1,256]{3,1,2,0:T(8,128)S(1)}, f32[3,6,1,256]{3,1,2,0:T(8,128)S(1)}, u32[]{:S(2)}, u32[]{:S(2)}) %collective-permute-start.8) | collective-permute-done | bytes 18464 | tf_op jit(solution)/shard_map/ppermute | solution.py:18
  188.9 4.3 %collective-permute-start.10 = (f32[3,6,34,1]{3,2,1,0:T(8,128)S(1)}, f32[3,6,34,1]{3,2,1,0:T(8,128)S(1)}, u32[]{:S(2)}, u32[]{:S(2)}) collective-permute-start(f32[3,6,34,1]{3,2,1,0:T(8,128)S(1)} %get-tuple-element.46), channel_id=1, source_target_pairs={{0,1},{1,2},{2,3},{3,4},{4,5},{5,6},{6,7},{8,9},{9,10},{10,11},{11... | collective-permute-start | bytes 7352 | tf_op jit(solution)/shard_map/ppermute | solution.py:18
  193.2 1.9 collective-permute-start.11
  195.2 2.4 collective-permute-done.10
  197.6 4.4 %collective-permute-done.11 = f32[3,6,34,1]{3,2,1,0:T(8,128)S(1)} collective-permute-done((f32[3,6,34,1]{3,2,1,0:T(8,128)S(1)}, f32[3,6,34,1]{3,2,1,0:T(8,128)S(1)}, u32[]{:S(2)}, u32[]{:S(2)}) %collective-permute-start.11) | collective-permute-done | bytes 2480 | tf_op jit(solution)/shard_map/ppermute | solution.py:21
  206.2 1.9 collective-permute-start.12
  208.1 3.4 %collective-permute-start.13 = (f32[3,1,32,256]{3,2,1,0:T(8,128)S(1)}, f32[3,1,32,256]{3,2,1,0:T(8,128)S(1)}, u32[]{:S(2)}, u32[]{:S(2)}) collective-permute-start(f32[3,1,32,256]{3,2,1,0:T(8,128)S(1)} %get-tuple-element.55), channel_id=1, source_target_pairs={{32,0},{64,32},{96,64},{128,96},{160,128},{192,160},{224,192},{33,... | collective-permute-start | bytes 294920 | tf_op jit(solution)/shard_map/ppermute | solution.py:21
  211.6 7.9 %collective-permute-done.13 = f32[3,1,32,256]{3,2,1,0:T(8,128)S(1)} collective-permute-done((f32[3,1,32,256]{3,2,1,0:T(8,128)S(1)}, f32[3,1,32,256]{3,2,1,0:T(8,128)S(1)}, u32[]{:S(2)}, u32[]{:S(2)}) %collective-permute-start.13) | collective-permute-done | bytes 98336 | tf_op jit(solution)/shard_map/ppermute | solution.py:21
  219.5 2.7 %collective-permute-start.15 = (f32[3,6,1,256]{3,1,2,0:T(8,128)S(1)}, f32[3,6,1,256]{3,1,2,0:T(8,128)S(1)}, u32[]{:S(2)}, u32[]{:S(2)}) collective-permute-start(f32[3,6,1,256]{3,1,2,0:T(8,128)S(1)} %copy.62), channel_id=1, source_target_pairs={{8,0},{16,8},{24,16},{9,1},{17,9},{25,17},{10,2},{18,10},{26,18},{... | collective-permute-start | bytes 55304 | tf_op jit(solution)/shard_map/ppermute | solution.py:21
  222.3 2.6 %collective-permute-start.14 = (f32[3,6,1,256]{3,1,2,0:T(8,128)S(1)}, f32[3,6,1,256]{3,1,2,0:T(8,128)S(1)}, u32[]{:S(2)}, u32[]{:S(2)}) collective-permute-start(f32[3,6,1,256]{3,1,2,0:T(8,128)S(1)} %copy.61), channel_id=1, source_target_pairs={{0,8},{8,16},{16,24},{1,9},{9,17},{17,25},{2,10},{10,18},{18,26},{... | collective-permute-start | bytes 55304 | tf_op jit(solution)/shard_map/ppermute | solution.py:18
  224.9 1.9 collective-permute-done.14
  226.9 1.9 collective-permute-start.16
  228.8 9.6 %collective-permute-done.16 = f32[3,6,34,1]{3,2,1,0:T(8,128)S(1)} collective-permute-done((f32[3,6,34,1]{3,2,1,0:T(8,128)S(1)}, f32[3,6,34,1]{3,2,1,0:T(8,128)S(1)}, u32[]{:S(2)}, u32[]{:S(2)}) %collective-permute-start.16) | collective-permute-done | bytes 2480 | tf_op jit(solution)/shard_map/ppermute | solution.py:21
  239.8 1.7 fusion.8
  241.5 1.8 fusion.44
  (125 shorter events, 13.5 us)
Async XLA Ops:
  0.6 26.4 %copy-start.7 = (f32[3,4,32,256]{3,2,1,0:T(8,128)S(1)}, f32[3,4,32,256]{3,2,1,0:T(8,128)}, u32[]{:S(2)}) copy-start(f32[3,4,32,256]{3,2,1,0:T(8,128)} %param.4) | copy-start | bytes 1179652
  3.7 13.2 %collective-permute-start = (f32[5,1,32,256]{3,2,1,0:T(8,128)S(1)}, f32[5,1,32,256]{3,2,1,0:T(8,128)S(1)}, u32[]{:S(2)}, u32[]{:S(2)}) collective-permute-start(f32[5,1,32,256]{3,2,1,0:T(8,128)S(1)} %get-tuple-element.48), channel_id=1, source_target_pairs={{0,32},{32,64},{64,96},{96,128},{128,160},{160,192},{192,224},{1,3... | collective-permute-start | bytes 491528 | tf_op jit(solution)/shard_map/ppermute | solution.py:18
  10.4 16.7 %collective-permute-start.1 = (f32[5,1,32,256]{3,2,1,0:T(8,128)S(1)}, f32[5,1,32,256]{3,2,1,0:T(8,128)S(1)}, u32[]{:S(2)}, u32[]{:S(2)}) collective-permute-start(f32[5,1,32,256]{3,2,1,0:T(8,128)S(1)} %get-tuple-element.49), channel_id=1, source_target_pairs={{32,0},{64,32},{96,64},{128,96},{160,128},{192,160},{224,192},{33,... | collective-permute-start | bytes 491528 | tf_op jit(solution)/shard_map/ppermute | solution.py:21
  27.1 8.5 %collective-permute-start.2 = (f32[5,6,1,256]{3,1,2,0:T(8,128)S(1)}, f32[5,6,1,256]{3,1,2,0:T(8,128)S(1)}, u32[]{:S(2)}, u32[]{:S(2)}) collective-permute-start(f32[5,6,1,256]{3,1,2,0:T(8,128)S(1)} %copy.57), channel_id=1, source_target_pairs={{0,8},{8,16},{16,24},{1,9},{9,17},{17,25},{2,10},{10,18},{18,26},{... | collective-permute-start | bytes 92168 | tf_op jit(solution)/shard_map/ppermute | solution.py:18
  29.1 9.6 %collective-permute-start.3 = (f32[5,6,1,256]{3,1,2,0:T(8,128)S(1)}, f32[5,6,1,256]{3,1,2,0:T(8,128)S(1)}, u32[]{:S(2)}, u32[]{:S(2)}) collective-permute-start(f32[5,6,1,256]{3,1,2,0:T(8,128)S(1)} %copy.58), channel_id=1, source_target_pairs={{8,0},{16,8},{24,16},{9,1},{17,9},{25,17},{10,2},{18,10},{26,18},{... | collective-permute-start | bytes 92168 | tf_op jit(solution)/shard_map/ppermute | solution.py:21
  50.1 2.3 copy-start
  52.5 11.0 %collective-permute-start.4 = (f32[5,6,34,1]{2,1,3,0:T(8,128)S(1)}, f32[5,6,34,1]{2,1,3,0:T(8,128)S(1)}, u32[]{:S(2)}, u32[]{:S(2)}) collective-permute-start(f32[5,6,34,1]{2,1,3,0:T(8,128)S(1)} %get-tuple-element.24), channel_id=1, source_target_pairs={{0,1},{1,2},{2,3},{3,4},{4,5},{5,6},{6,7},{8,9},{9,10},{10,11},{11... | collective-permute-start | bytes 12248 | tf_op jit(solution)/shard_map/ppermute | solution.py:18
  61.6 5.1 %collective-permute-start.5 = (f32[5,6,34,1]{2,1,3,0:T(8,128)S(1)}, f32[5,6,34,1]{2,1,3,0:T(8,128)S(1)}, u32[]{:S(2)}, u32[]{:S(2)}) collective-permute-start(f32[5,6,34,1]{2,1,3,0:T(8,128)S(1)} %get-tuple-element.23), channel_id=1, source_target_pairs={{1,0},{2,1},{3,2},{4,3},{5,4},{6,5},{7,6},{9,8},{10,9},{11,10},{12... | collective-permute-start | bytes 12248 | tf_op jit(solution)/shard_map/ppermute | solution.py:21
  68.8 0.9 copy-start.4
  69.2 1.0 copy-start.2
  69.5 1.9 copy-start.3
  69.5 1.9 copy-start.12
  70.2 2.7 %copy-start.6 = (f32[4,33,257]{2,1,0:T(8,128)S(1)}, f32[4,33,257]{2,1,0:T(8,128)}, u32[]{:S(2)}) copy-start(f32[4,33,257]{2,1,0:T(8,128)} %fusion.38) | copy-start | bytes 407092
  71.4 0.8 copy-start.11
  150.0 5.8 %copy-start.5 = (f32[1,5,33,257]{3,2,1,0:T(8,128)S(1)}, f32[1,5,33,257]{3,2,1,0:T(8,128)}, u32[]{:S(2)}) copy-start(f32[1,5,33,257]{3,2,1,0:T(8,128)} %get-tuple-element.18) | copy-start | bytes 508864
  150.0 5.8 %copy-start.8 = (f32[1,5,33,257]{3,2,1,0:T(8,128)S(1)}, f32[1,5,33,257]{3,2,1,0:T(8,128)}, u32[]{:S(2)}) copy-start(f32[1,5,33,257]{3,2,1,0:T(8,128)} %get-tuple-element.19) | copy-start | bytes 508864
  158.4 0.9 copy-start.10
  158.4 1.0 copy-start.13
  159.8 7.0 %collective-permute-start.6 = (f32[3,1,32,256]{3,2,1,0:T(8,128)S(1)}, f32[3,1,32,256]{3,2,1,0:T(8,128)S(1)}, u32[]{:S(2)}, u32[]{:S(2)}) collective-permute-start(f32[3,1,32,256]{3,2,1,0:T(8,128)S(1)} %get-tuple-element.56), channel_id=1, source_target_pairs={{0,32},{32,64},{64,96},{96,128},{128,160},{160,192},{192,224},{1,3... | collective-permute-start | bytes 294920 | tf_op jit(solution)/shard_map/ppermute | solution.py:18
  164.9 11.4 %collective-permute-start.7 = (f32[3,1,32,256]{3,2,1,0:T(8,128)S(1)}, f32[3,1,32,256]{3,2,1,0:T(8,128)S(1)}, u32[]{:S(2)}, u32[]{:S(2)}) collective-permute-start(f32[3,1,32,256]{3,2,1,0:T(8,128)S(1)} %get-tuple-element.57), channel_id=1, source_target_pairs={{32,0},{64,32},{96,64},{128,96},{160,128},{192,160},{224,192},{33,... | collective-permute-start | bytes 294920 | tf_op jit(solution)/shard_map/ppermute | solution.py:21
  176.3 9.6 %collective-permute-start.9 = (f32[3,6,1,256]{3,1,2,0:T(8,128)S(1)}, f32[3,6,1,256]{3,1,2,0:T(8,128)S(1)}, u32[]{:S(2)}, u32[]{:S(2)}) collective-permute-start(f32[3,6,1,256]{3,1,2,0:T(8,128)S(1)} %copy.60), channel_id=1, source_target_pairs={{8,0},{16,8},{24,16},{9,1},{17,9},{25,17},{10,2},{18,10},{26,18},{... | collective-permute-start | bytes 55304 | tf_op jit(solution)/shard_map/ppermute | solution.py:21
  184.0 4.6 %collective-permute-start.8 = (f32[3,6,1,256]{3,1,2,0:T(8,128)S(1)}, f32[3,6,1,256]{3,1,2,0:T(8,128)S(1)}, u32[]{:S(2)}, u32[]{:S(2)}) collective-permute-start(f32[3,6,1,256]{3,1,2,0:T(8,128)S(1)} %copy.59), channel_id=1, source_target_pairs={{0,8},{8,16},{16,24},{1,9},{9,17},{17,25},{2,10},{10,18},{18,26},{... | collective-permute-start | bytes 55304 | tf_op jit(solution)/shard_map/ppermute | solution.py:18
  188.9 8.7 %collective-permute-start.10 = (f32[3,6,34,1]{3,2,1,0:T(8,128)S(1)}, f32[3,6,34,1]{3,2,1,0:T(8,128)S(1)}, u32[]{:S(2)}, u32[]{:S(2)}) collective-permute-start(f32[3,6,34,1]{3,2,1,0:T(8,128)S(1)} %get-tuple-element.46), channel_id=1, source_target_pairs={{0,1},{1,2},{2,3},{3,4},{4,5},{5,6},{6,7},{8,9},{9,10},{10,11},{11... | collective-permute-start | bytes 7352 | tf_op jit(solution)/shard_map/ppermute | solution.py:18
  193.2 8.8 %collective-permute-start.11 = (f32[3,6,34,1]{3,2,1,0:T(8,128)S(1)}, f32[3,6,34,1]{3,2,1,0:T(8,128)S(1)}, u32[]{:S(2)}, u32[]{:S(2)}) collective-permute-start(f32[3,6,34,1]{3,2,1,0:T(8,128)S(1)} %get-tuple-element.47), channel_id=1, source_target_pairs={{1,0},{2,1},{3,2},{4,3},{5,4},{6,5},{7,6},{9,8},{10,9},{11,10},{12... | collective-permute-start | bytes 7352 | tf_op jit(solution)/shard_map/ppermute | solution.py:21
  206.2 32.6 %copy-start.1 = (f32[3,4,32,256]{3,2,1,0:T(8,128)}, f32[3,4,32,256]{3,2,1,0:T(8,128)S(1)}, u32[]{:S(2)}) copy-start(f32[3,4,32,256]{3,2,1,0:T(8,128)S(1)} %fusion.19) | copy-start | bytes 1179652
  206.2 5.4 %collective-permute-start.12 = (f32[3,1,32,256]{3,2,1,0:T(8,128)S(1)}, f32[3,1,32,256]{3,2,1,0:T(8,128)S(1)}, u32[]{:S(2)}, u32[]{:S(2)}) collective-permute-start(f32[3,1,32,256]{3,2,1,0:T(8,128)S(1)} %get-tuple-element.54), channel_id=1, source_target_pairs={{0,32},{32,64},{64,96},{96,128},{128,160},{160,192},{192,224},{1,3... | collective-permute-start | bytes 294920 | tf_op jit(solution)/shard_map/ppermute | solution.py:18
  208.1 11.4 %collective-permute-start.13 = (f32[3,1,32,256]{3,2,1,0:T(8,128)S(1)}, f32[3,1,32,256]{3,2,1,0:T(8,128)S(1)}, u32[]{:S(2)}, u32[]{:S(2)}) collective-permute-start(f32[3,1,32,256]{3,2,1,0:T(8,128)S(1)} %get-tuple-element.55), channel_id=1, source_target_pairs={{32,0},{64,32},{96,64},{128,96},{160,128},{192,160},{224,192},{33,... | collective-permute-start | bytes 294920 | tf_op jit(solution)/shard_map/ppermute | solution.py:21
  219.5 5.3 %collective-permute-start.15 = (f32[3,6,1,256]{3,1,2,0:T(8,128)S(1)}, f32[3,6,1,256]{3,1,2,0:T(8,128)S(1)}, u32[]{:S(2)}, u32[]{:S(2)}) collective-permute-start(f32[3,6,1,256]{3,1,2,0:T(8,128)S(1)} %copy.62), channel_id=1, source_target_pairs={{8,0},{16,8},{24,16},{9,1},{17,9},{25,17},{10,2},{18,10},{26,18},{... | collective-permute-start | bytes 55304 | tf_op jit(solution)/shard_map/ppermute | solution.py:21
  222.3 4.6 %collective-permute-start.14 = (f32[3,6,1,256]{3,1,2,0:T(8,128)S(1)}, f32[3,6,1,256]{3,1,2,0:T(8,128)S(1)}, u32[]{:S(2)}, u32[]{:S(2)}) collective-permute-start(f32[3,6,1,256]{3,1,2,0:T(8,128)S(1)} %copy.61), channel_id=1, source_target_pairs={{0,8},{8,16},{16,24},{1,9},{9,17},{17,25},{2,10},{10,18},{18,26},{... | collective-permute-start | bytes 55304 | tf_op jit(solution)/shard_map/ppermute | solution.py:18
  226.9 11.5 %collective-permute-start.16 = (f32[3,6,34,1]{3,2,1,0:T(8,128)S(1)}, f32[3,6,34,1]{3,2,1,0:T(8,128)S(1)}, u32[]{:S(2)}, u32[]{:S(2)}) collective-permute-start(f32[3,6,34,1]{3,2,1,0:T(8,128)S(1)} %pad_maximum_fusion.16), channel_id=1, source_target_pairs={{1,0},{2,1},{3,2},{4,3},{5,4},{6,5},{7,6},{9,8},{10,9},{11,10},{12... | collective-permute-start | bytes 7352 | tf_op jit(solution)/shard_map/ppermute | solution.py:21
  239.6 1.8 copy-start.9
where the time goes:
time: 244 us; the launch traced here: 243 us
  blocking collectives  72.1 us (30%)
  starting transfers between devices  56 us (23%)
  waiting for transfers between devices  55 us (23%)
  other arithmetic  39.4 us (16%)
  local copies, waits for them, and re-layouts  18.6 us (8%)
    psum x1, blocking collectives, per_device(): global_sum = lax.psum(partial_value, ('gx', 'gy', 'gz'))  72.1 us
    ppermute x9, waiting for transfers between devices, padded(): lax.ppermute(lax.slice_in_dim(block, 0, width, axis=dim), axis, backward)  43.4 us
    ppermute x8, starting transfers between devices, padded(): lax.ppermute(lax.slice_in_dim(block, block.shape[dim] - width, None, axis...  29.3 us
    ppermute x9, starting transfers between devices, padded(): lax.ppermute(lax.slice_in_dim(block, 0, width, axis=dim), axis, backward)  26.7 us
    ppermute x8, waiting for transfers between devices, padded(): lax.ppermute(lax.slice_in_dim(block, block.shape[dim] - width, None, axis...  11.6 us
    concatenate x7, other arithmetic, padded(): block = jnp.concatenate([low, block, high], axis=dim)  9.93 us
    unnamed x15, other arithmetic  8.85 us
    concatenate x2, local copies, waits for them, and re-layouts, padded(): block = jnp.concatenate([low, block, high], axis=dim)  7.31 us
  transfers between devices with their start and end apart: 17, of which 11 were waited for; matrix products, arithmetic and copies ran while one was open for 5% of the time, Pallas kernels for 0%

commit v1 on v0

v1 whole, which is shorter than its diff:
```python
import functools
import itertools

import jax
import jax.numpy as jnp
from jax import lax
from jax.experimental import pallas as pl
from jax.experimental.pallas import tpu as pltpu
from jax.sharding import PartitionSpec as P

LAM = 0.577
MU = 0.385
DIAG = (0.577 + 4.0 * 0.385) / 16.0
RELAX = 0.6
SHIFT = 1e-06
BOOST = 2.0**18
MESH = pl.DeviceIdType.MESH
F32 = jnp.float32
ROWS = 48
SIDES = [d for d in itertools.product((-1, 0, 1), repeat=2) if d != (0, 0)]
TILES = [d for d in itertools.product((-1, 0, 1), repeat=3) if d != (0, 0, 0)]
LAST_SIDES = [(-1, 0), (0, -1), (-1, -1)]
LAST_TILES = [(dx, dy, -1) for dx in (0, -1) for dy in (0, -1)]


def span(step):
    return {1: (slice(4, 5), slice(0, 1)), -1: (slice(1, 2), slice(5, 6)), 0: (slice(1, 5), slice(1, 5))}[step]


def rows_of(step):
    return {1: (slice(39, 40), slice(7, 8)), -1: (slice(8, 9), slice(40, 41)), 0: (slice(8, 40), slice(8, 40))}[step]


def kernel(sizes, disp, dens, mat, fix, adj_out, sens_out, *scratch):
    (U, FI, AD, DN, MT, FX, PS, QS, R6, KF, S0, SE, FD, TS, TR, PL, PK, WP, SUM, in_sem,
     f1s, f1r, t1s, t1r, f2s, f2r, t2s, t2r, f3s, f3r, t3s, t3r, ass, asr) = scratch
    nx, ny, nz = sizes
    count = nx * ny * nz * 4 * 32 * 256
    me = (lax.axis_index("gx"), lax.axis_index("gy"), lax.axis_index("gz"))
    lane = lax.broadcasted_iota(jnp.int32, (8, 128), 1)
    first_lane = lane == 0
    last_lane = lane == 127

    def exists(step):
        ok = None
        for i, s, n in zip(me, step, sizes):
            if s:
                one = i < n - 1 if s > 0 else i > 0
                ok = one if ok is None else jnp.logical_and(ok, one)
        return ok

    def at(step):
        return tuple(i + s for i, s in zip(me, step))

    def back(step):
        return tuple(-s for s in step)

    loads = []
    for lt in range(2):
        cols = pl.ds(lt * 128, 128)
        loads.append(pltpu.make_async_copy(disp.at[:, :, :, cols], U.at[0:3, 1:5, lt, 8:40, :], in_sem.at[4 * lt]))
        loads.append(pltpu.make_async_copy(dens.at[:, :, cols], DN.at[:, lt], in_sem.at[4 * lt + 1]))
        loads.append(pltpu.make_async_copy(mat.at[:, :, cols], MT.at[:, lt], in_sem.at[4 * lt + 2]))
        loads.append(pltpu.make_async_copy(fix.at[:, :, cols], FX.at[:, lt], in_sem.at[4 * lt + 3]))
    for c in loads:
        c.start()

    barrier = pltpu.get_barrier_semaphore()

    def greet(device):
        pl.semaphore_signal(barrier, inc=1, device_id=device, device_id_type=MESH)

    for step in TILES:
        pl.when(exists(step))(functools.partial(greet, at(step)))
    rings = []
    for axis, n in enumerate(sizes):
        for k in range(1, n):
            peer = list(me)
            peer[axis] = lax.rem(me[axis] + k, n)
            rings.append((axis, k, tuple(peer)))
            greet(tuple(peer))

    def clear(ref, comps, tile):
        for step, where in (((-1, 0, 0), 0), ((1, 0, 0), 5)):
            def fill(where=where):
                for c in range(comps):
                    for lt in range(2):
                        ref[c, where, lt, 7:41, :] = jnp.full((34, 128), -1.0 if c == 3 else 0.0, F32)
            pl.when(jnp.logical_not(exists(step)))(fill)
        for step, row in (((0, -1, 0), 7), ((0, 1, 0), 40)):
            def fill(row=row):
                for c in range(comps):
                    for x in range(6):
                        for lt in range(2):
                            ref[c, x, lt, row : row + 1, :] = jnp.full((1, 128), -1.0 if c == 3 else 0.0, F32)
            pl.when(jnp.logical_not(exists(step)))(fill)
        for step in TILES:
            def fill(step=step):
                tile[slot(step)] = jnp.where(lane % 32 >= 24, -1.0, 0.0)
            pl.when(jnp.logical_not(exists(back(step))))(fill)

    def slot(step):
        return ((1 - step[2]) * 3 + step[0] + 1) * 3 + step[1] + 1

    clear(U, 4, TR.at[0])
    clear(FI, 3, TR.at[1])
    clear(AD, 3, TR.at[2])
    for c in loads:
        c.wait()

    for x in range(4):
        for lt in range(2):
            m = MT[x, lt]
            U[3, x + 1, lt, 8:40, :] = jnp.where(m == 1, DN[x, lt], jnp.where(m == 2, 1.0, 0.0))

    def pack(ref, comps, high):
        lt, source = (1, 127) if high else (0, 0)
        parts = []
        for g in range(4):
            part = jnp.zeros((8, 128), F32)
            for c in range(comps):
                for x in range(1, 5):
                    to = 32 * g + 8 * c + x
                    v = ref[c, x, lt, 8 + 8 * g : 16 + 8 * g, :]
                    part = jnp.where(lane == to, pltpu.roll(v, (to - source) % 128, 1), part)
            parts.append(part)
        return (parts[0] + parts[1]) + (parts[2] + parts[3])

    def sides(ref, steps, comps_of, send, recv):
        out = []
        for i, (dx, dy) in enumerate(steps):
            (sx, tx), (sr, tr) = span(dx), rows_of(dy)
            comps = slice(0, comps_of(dx, dy))
            out.append(((dx, dy, 0), pltpu.make_async_remote_copy(
                src_ref=ref.at[comps, sx, :, sr, :], dst_ref=ref.at[comps, tx, :, tr, :],
                send_sem=send.at[i], recv_sem=recv.at[i], device_id=at((dx, dy, 0)), device_id_type=MESH)))
        return out

    def tiles(k, steps, send, recv):
        out = []
        for i, step in enumerate(steps):
            out.append((step, pltpu.make_async_remote_copy(
                src_ref=TS.at[k, 1 if step[2] > 0 else 0], dst_ref=TR.at[k, slot(step)],
                send_sem=send.at[i], recv_sem=recv.at[i], device_id=at(step), device_id_type=MESH)))
        return out

    def start(copies):
        for step, c in copies:
            pl.when(exists(step))(c.start)

    def arrive(copies):
        for step, c in copies:
            pl.when(exists(back(step)))(c.wait_recv)

    def left(copies):
        for step, c in copies:
            pl.when(exists(step))(c.wait_send)

    def merge(k, plane, own):
        def tile(dx, dy):
            if plane == 1 and (dx, dy) == (0, 0):
                return own
            return TR[k, (plane * 3 + dx + 1) * 3 + dy + 1]
        for dy in (-1, 0, 1):
            low, mid, high = tile(1, dy), tile(0, dy), tile(-1, dy)
            full = jnp.where(lane % 8 == 0, pltpu.roll(low, 124, 1), jnp.where(lane % 8 == 5, pltpu.roll(high, 4, 1), mid))
            if dy == 0:
                for g in range(4):
                    PL[plane, 8 + 8 * g : 16 + 8 * g, :] = pltpu.roll(full, (128 - 32 * g) % 128, 1) if g else full
            elif dy == 1:
                PL[plane, 0:8, :] = pltpu.roll(full, 32, 1)
            else:
                PL[plane, 40:48, :] = full

    def sweep_z(ref, x_from):
        def body(g, carry):
            rows = pl.ds(7 + 8 * g, 8)
            edge = PL[2, rows, :]
            for c in range(3):
                for x in range(x_from, 6):
                    t0, t1 = ref[c, x, 0, rows, :], ref[c, x, 1, rows, :]
                    r0, r1 = pltpu.roll(t0, 127, 1), pltpu.roll(t1, 127, 1)
                    s0 = jnp.where(last_lane, r1, r0)
                    s1 = jnp.where(last_lane, pltpu.roll(edge, (127 - 8 * c - x) % 128, 1), r1)
                    PS[c, x, 0, rows, :] = s0 + t0
                    PS[c, x, 1, rows, :] = s1 + t1
                    QS[c, x, 0, rows, :] = s0 - t0
                    QS[c, x, 1, rows, :] = s1 - t1
            return carry
        lax.fori_loop(0, 5, body, 0)

    def gradients(low, high):
        return [[high[c][0] - low[c][0] for c in range(3)], [high[c][1] + low[c][1] for c in range(3)],
                [high[c][2] + low[c][2] for c in range(3)]]

    def strain6(g):
        gx, gy, gz = g
        return gx[0], gy[1], gz[2], gy[0] + gx[1], gz[1] + gy[2], gx[2] + gz[0]

    def y_sums(x, lt, base):
        out = []
        for c in range(3):
            p0, p1 = PS[c, x, lt, pl.ds(base, 8), :], PS[c, x, lt, pl.ds(base + 1, 8), :]
            q0, q1 = QS[c, x, lt, pl.ds(base, 8), :], QS[c, x, lt, pl.ds(base + 1, 8), :]
            out.append((p0 + p1, p1 - p0, q0 + q1))
        return out

    def packed_strain(k):
        lo, hi = PL[0], PL[1]
        PK[0] = lo + hi
        PK[1] = hi - lo
        p0, p1, q0, q1 = PK[0, 0:40], PK[0, 1:41], PK[1, 0:40], PK[1, 1:41]
        a, b, c = p0 + p1, p1 - p0, q0 + q1
        g = [pltpu.roll(a, 127, 1) - a, pltpu.roll(b, 127, 1) + b, pltpu.roll(c, 127, 1) + c]
        return strain6([[t] + [pltpu.roll(t, 128 - 8 * i, 1) for i in (1, 2)] for t in g])

    def load_terms(e, d):
        a, b, c = e[0] - e[1], e[1] - e[2], e[2] - e[0]
        q = (MU * MU / 16.0) * (2.0 * (a * a + b * b + c * c) + 3.0 * (e[3] * e[3] + e[4] * e[4] + e[5] * e[5]))
        vm = d * q
        w = vm * vm * vm
        t = (-MU * MU / 8.0 * BOOST) * (w * d)
        ts = 1.5 * t
        return q, vm, w, (t * (a - c), t * (b - a), t * (c - b), ts * e[3], ts * e[4], ts * e[5])

    def stiff_terms(e, kf):
        k = kf * (-2.0 * MU / 16.0)
        tr = (kf * (-LAM / 16.0)) * (e[0] + e[1] + e[2])
        ks = kf * (-MU / 16.0)
        return tr + k * e[0], tr + k * e[1], tr + k * e[2], ks * e[3], ks * e[4], ks * e[5]

    S_Y, D_Y = (0, 3, 5, 4, 2), (3, 1, 4)

    def x_parts(low, high):
        (sl, dl), (sh, dh) = low, high
        return [((sh[i] - sl[i]) + (dh[j] + dl[j]), sh[k] + sl[k]) for i, j, k in ((0, 3, 5), (3, 1, 4), (5, 4, 2))]

    def packed_forces(r):
        for i in range(6):
            PK[i, 0:40] = r[i]
        s = {i: PK[i, 7:39] + PK[i, 8:40] for i in S_Y}
        d = {i: PK[i, 8:40] - PK[i, 7:39] for i in D_Y}
        high = ({i: pltpu.roll(v, 127, 1) for i, v in s.items()}, {i: pltpu.roll(v, 127, 1) for i, v in d.items()})
        for c, (u, w) in enumerate(x_parts((s, d), high)):
            WP[c] = u - w

    def from_low(w0, w1, packed, x):
        r0, r1 = pltpu.roll(w0, 1, 1), pltpu.roll(w1, 1, 1)
        edge = pltpu.roll(packed, (128 - x) % 128, 1) if x else packed
        return jnp.where(first_lane, edge, r0), jnp.where(first_lane, r0, r1)

    def forces(finish):
        def body(g, carry):
            base = pl.multiple_of(8 + 8 * g, 8)
            own = pl.ds(pl.multiple_of(8 * g, 8), 8)
            packed = [WP[c, own, :] for c in range(3)]

            def sums(x):
                out = []
                for lt in range(2):
                    r1 = [R6[i, x, lt, pl.ds(base, 8), :] for i in range(6)]
                    r0 = [R6[i, x, lt, pl.ds(base - 1, 8), :] for i in range(6)]
                    out.append(({i: r0[i] + r1[i] for i in S_Y}, {i: r1[i] - r0[i] for i in D_Y}))
                return out

            low = sums(0)
            for x in range(4):
                high = sums(x + 1)
                p0, p1 = x_parts(low[0], high[0]), x_parts(low[1], high[1])
                for c in range(3):
                    (u0, c0), (u1, c1) = p0[c], p1[c]
                    s0, s1 = from_low(u0 - c0, u1 - c1, packed[c], x)
                    finish(c, x, 0, base, own, u0 + c0 + s0)
                    finish(c, x, 1, base, own, u1 + c1 + s1)
                low = high
            return carry
        lax.fori_loop(0, 4, body, 0)

    own_tile = pack(U, 4, False)
    TS[0, 0] = own_tile
    TS[0, 1] = pack(U, 4, True)

    block = 1
    for i, n in zip(me, sizes):
        block = block * (1 + (i > 0).astype(jnp.int32) + (i < n - 1).astype(jnp.int32))
    pl.semaphore_wait(barrier, block - 1 + len(rings))

    t1 = tiles(0, TILES, t1s, t1r)
    f1 = sides(U, SIDES, lambda dx, dy: 4 if dx >= 0 and dy >= 0 else 3, f1s, f1r)
    start(t1)
    start(f1)
    arrive(t1)
    arrive(f1)

    for plane in range(3):
        merge(0, plane, own_tile)
    d = pltpu.roll(PL[0, 0:40, :], 104, 1)
    kp = jnp.where(d < 0.0, 0.0, 0.001 + d * d * d)
    e = packed_strain(0)
    r = load_terms(e, jnp.maximum(d, 0.0))[3]
    packed_forces(r)
    PK[6, 0:40] = kp
    ky = PK[6, 7:39] + PK[6, 8:40]
    WP[3] = ky + pltpu.roll(ky, 127, 1)
    sweep_z(U, 0)

    def power_body(g, total):
        base = pl.multiple_of(8 * g, 8)
        rows = pl.ds(base, 8)
        own = pl.ds(pl.multiple_of(jnp.maximum(8 * g - 8, 0), 8), 8)
        inside = (g > 0).astype(F32)
        for lt in range(2):
            low = y_sums(0, lt, base)
            for x in range(5):
                high = y_sums(x + 1, lt, base)
                e = strain6(gradients(low, high))
                low = high
                d = U[3, x, lt, rows, :]
                KF[x, lt, rows, :] = jnp.where(d < 0.0, 0.0, 0.001 + d * d * d)
                q, vm, w, r = load_terms(e, jnp.maximum(d, 0.0))
                for i in range(6):
                    R6[i, x, lt, rows, :] = r[i]
                if x > 0:
                    v2 = vm * vm
                    total = total + jnp.where(inside > 0.0, v2 * v2, 0.0)
                    tr = (LAM / 16.0) * (e[0] + e[1] + e[2])
                    for i in range(6):
                        S0[i, x - 1, lt, own, :] = tr + (MU / 8.0) * e[i] if i < 3 else (MU / 16.0) * e[i]
                    design = MT[x - 1, lt, own, :] == 1
                    SE[x - 1, lt, own, :] = jnp.where(design, (0.5 * BOOST) * (w * q), 0.0)
        return total

    total = lax.fori_loop(0, 5, power_body, jnp.zeros((8, 128), F32))

    order = (2, 1, 0)

    def ring(stage):
        axis, out = order[stage], []
        for i, (a, k, peer) in enumerate(rings):
            if a == axis:
                out.append(pltpu.make_async_remote_copy(
                    src_ref=SUM.at[stage, me[axis]], dst_ref=SUM.at[stage, me[axis]],
                    send_sem=ass.at[i], recv_sem=asr.at[i], device_id=peer, device_id_type=MESH))
        return out

    def send_sum(stage, value):
        SUM[stage, me[order[stage]]] = value
        for c in ring(stage):
            c.start()

    def take_sum(stage):
        for c in ring(stage):
            c.wait_recv()
        value = SUM[stage, 0]
        for i in range(1, sizes[order[stage]]):
            value = value + SUM[stage, i]
        return value

    send_sum(0, total)

    def diag_body(g, carry):
        base = pl.multiple_of(8 + 8 * g, 8)
        own = pl.ds(pl.multiple_of(8 * g, 8), 8)
        packed = WP[3, own, :]

        def sums(x):
            return [KF[x, lt, pl.ds(base, 8), :] + KF[x, lt, pl.ds(base - 1, 8), :] for lt in range(2)]

        low = sums(0)
        for x in range(4):
            high = sums(x + 1)
            k0, k1 = low[0] + high[0], low[1] + high[1]
            s0, s1 = from_low(k0, k1, packed, x)
            for lt, k in ((0, k0 + s0), (1, k1 + s1)):
                fixed = FX[x, lt, own, :].astype(F32)
                FD[x, lt, own, :] = (1.0 - fixed) / (DIAG * k + fixed)
            low = high
        return carry

    lax.fori_loop(0, 4, diag_body, 0)

    def first_out(c, x, lt, base, own, value):
        FI[c, x + 1, lt, pl.ds(base, 8), :] = value * FD[x, lt, own, :]

    forces(first_out)

    own_tile = pack(FI, 3, False)
    TS[1, 0] = own_tile
    TS[1, 1] = pack(FI, 3, True)
    t2 = tiles(1, TILES, t2s, t2r)
    f2 = sides(FI, SIDES, lambda dx, dy: 3, f2s, f2r)
    start(t2)
    start(f2)
    send_sum(1, take_sum(0))
    arrive(t2)
    arrive(f2)
    for plane in range(3):
        merge(1, plane, own_tile)
    packed_forces_in = packed_strain(1)
    packed_forces(stiff_terms(packed_forces_in, kp))
    sweep_z(FI, 0)

    def stiff_body(g, carry):
        base = pl.multiple_of(8 * g, 8)
        rows = pl.ds(base, 8)
        for lt in range(2):
            low = y_sums(0, lt, base)
            for x in range(5):
                high = y_sums(x + 1, lt, base)
                r = stiff_terms(strain6(gradients(low, high)), KF[x, lt, rows, :])
                low = high
                for i in range(6):
                    R6[i, x, lt, rows, :] = r[i]
        return carry

    lax.fori_loop(0, 5, stiff_body, 0)
    send_sum(2, take_sum(1))

    def adjoint_out(c, x, lt, base, own, value):
        AD[c, x + 1, lt, pl.ds(base, 8), :] = (1.0 + RELAX) * FI[c, x + 1, lt, pl.ds(base, 8), :] - RELAX * FD[x, lt, own, :] * value

    forces(adjoint_out)

    TS[2, 0] = pack(AD, 3, False)
    t3 = tiles(2, LAST_TILES, t3s, t3r)
    f3 = sides(AD, LAST_SIDES, lambda dx, dy: 3, f3s, f3r)
    start(t3)
    start(f3)
    arrive(t3)
    arrive(f3)
    merge(2, 2, None)
    sweep_z(AD, 1)

    total = jnp.sum(take_sum(2)) * (1.0 / count) + SHIFT
    total = jnp.full((8, 128), total, F32)
    scale = jnp.sqrt(jnp.sqrt(jnp.sqrt(total))) / total * (1.0 / BOOST)

    def last_body(g, carry):
        base = pl.multiple_of(8 + 8 * g, 8)
        rows = pl.ds(base, 8)
        own = pl.ds(pl.multiple_of(8 * g, 8), 8)
        for lt in range(2):
            cols = slice(128 * lt, 128 * lt + 128)
            low = y_sums(1, lt, base)
            for x in range(4):
                high = y_sums(x + 2, lt, base)
                e = strain6(gradients(low, high))
                low = high
                dot = e[0] * S0[0, x, lt, own, :]
                for i in range(1, 6):
                    dot = dot + e[i] * S0[i, x, lt, own, :]
                d = U[3, x + 1, lt, rows, :]
                slope = jnp.where(MT[x, lt, own, :] == 1, 3.0 * (d * d), 0.0)
                sens_out[x, own, cols] = scale * (SE[x, lt, own, :] - slope * dot)
                for c in range(3):
                    adj_out[c, x, own, cols] = scale * AD[c, x + 1, lt, rows, :]
        return carry

    lax.fori_loop(0, 4, last_body, 0)
    for copies in (t1, f1, t2, f2, t3, f3):
        left(copies)
    for stage in range(3):
        for c in ring(stage):
            c.wait_send()


def solution(mesh):
    sizes = tuple(mesh.shape[a] for a in ("gx", "gy", "gz"))
    peers = sum(sizes) - 3

    def per_device(displacement, density, material, fixed_mask):
        dma = pltpu.SemaphoreType.DMA
        return pl.pallas_call(
            functools.partial(kernel, sizes),
            out_shape=(jax.ShapeDtypeStruct((3, 4, 32, 256), F32), jax.ShapeDtypeStruct((4, 32, 256), F32)),
            in_specs=[pl.BlockSpec(memory_space=pl.ANY)] * 4,
            out_specs=[pl.BlockSpec(memory_space=pltpu.VMEM)] * 2,
            scratch_shapes=[
                pltpu.VMEM((4, 6, 2, ROWS, 128), F32),
                pltpu.VMEM((3, 6, 2, ROWS, 128), F32),
                pltpu.VMEM((3, 6, 2, ROWS, 128), F32),
                pltpu.VMEM((4, 2, 32, 128), F32),
                pltpu.VMEM((4, 2, 32, 128), jnp.int32),
                pltpu.VMEM((4, 2, 32, 128), jnp.int32),
                pltpu.VMEM((3, 6, 2, ROWS, 128), F32),
                pltpu.VMEM((3, 6, 2, ROWS, 128), F32),
                pltpu.VMEM((6, 5, 2, ROWS, 128), F32),
                pltpu.VMEM((5, 2, ROWS, 128), F32),
                pltpu.VMEM((6, 4, 2, 32, 128), F32),
                pltpu.VMEM((4, 2, 32, 128), F32),
                pltpu.VMEM((4, 2, 32, 128), F32),
                pltpu.VMEM((3, 2, 8, 128), F32),
                pltpu.VMEM((3, 27, 8, 128), F32),
                pltpu.VMEM((3, ROWS, 128), F32),
                pltpu.VMEM((7, ROWS, 128), F32),
                pltpu.VMEM((4, 32, 128), F32),
                pltpu.VMEM((3, 8, 8, 128), F32),
                dma((8,)),
                dma((8,)), dma((8,)), dma((26,)), dma((26,)),
                dma((8,)), dma((8,)), dma((26,)), dma((26,)),
                dma((3,)), dma((3,)), dma((4,)), dma((4,)),
                dma((peers,)), dma((peers,)),
            ],
            compiler_params=pltpu.CompilerParams(collective_id=0, has_side_effects=True),
        )(displacement, density, material, fixed_mask)

    placed = (P(None, "gx", "gy", "gz"), P("gx", "gy", "gz"), P("gx", "gy", "gz"), P("gx", "gy", "gz"))
    return jax.shard_map(per_device, mesh=mesh, in_specs=placed, out_specs=(placed[0], placed[1]), check_vma=False)
```

time: 244 us -> 47.6 us (0.20)
  the two profiles are of different devices: /device:TPU:89 before, /device:TPU:57 now
where the time goes in v1:
time: 47.6 us; the launch traced here: 47.5 us
  Pallas kernels  44.4 us (93%)
  local copies, waits for them, and re-layouts  2.46 us (5%)
  between operations  0.65 us (1%)
    pallas_call x1, Pallas kernels, per_device(): pl.pallas_call(functools.partial(kernel, sizes), out_shape=(jax.ShapeDtyp...  44.4 us
    unnamed x4, local copies, waits for them, and re-layouts  2.46 us

profile of v1, /device:TPU:57, one launch (start us, length us, event | category | flops | bytes accessed | tf_op | source)
XLA Modules:
  0.0 47.5 jit_solution(4339742412784327917)
XLA Ops:
  0.6 44.4 %shard_map.59 = (f32[3,4,32,256]{3,2,1,0:T(8,128)}, f32[4,32,256]{2,1,0:T(8,128)}) custom-call(f32[3,4,32,256]{3,2,1,0:T(8,128)} %disp.1, f32[4,32,256]{2,1,0:T(8,128)} %dens.1, s32[4,32,256]{2,1,0:T(8,128)} %mat.1, s32[4,32,256]{2,1,0:T(8,128)} %fix.1), custom_call_target="tpu_custom_call" | custom-call | tf_op jit(solution)/shard_map/pallas_call | solution.py:473
  45.0 0.0 copy-start
  45.0 1.8 %copy.8 = f32[3,4,32,256]{3,2,1,0:T(8,128)} copy(f32[3,4,32,256]{3,2,1,0:T(8,128)} %get-tuple-element.4) | data formatting | bytes 786432
  46.8 0.0 copy-done
  46.8 0.7 %copy.9 = f32[4,32,256]{2,1,0:T(8,128)} copy(f32[4,32,256]{2,1,0:T(8,128)S(1)} %copy-done) | data formatting | bytes 262144
Async XLA Ops:
  45.0 1.8 %copy-start = (f32[4,32,256]{2,1,0:T(8,128)S(1)}, f32[4,32,256]{2,1,0:T(8,128)}, u32[]{:S(2)}) copy-start(f32[4,32,256]{2,1,0:T(8,128)} %get-tuple-element.5) | copy-start | bytes 393220

commit v2 on v1

v2 whole, which is shorter than its diff:
```python
import functools
import itertools

import jax
import jax.numpy as jnp
from jax import lax
from jax.experimental import pallas as pl
from jax.experimental.pallas import tpu as pltpu
from jax.sharding import PartitionSpec as P

LAM = 0.577
MU = 0.385
DIAG = (0.577 + 4.0 * 0.385) / 16.0
RELAX = 0.6
SHIFT = 1e-06
BOOST = 2.0**18
MESH = pl.DeviceIdType.MESH
F32 = jnp.float32
ROWS = 48
NEAR = [d for d in itertools.product((-1, 0, 1), repeat=3) if d != (0, 0, 0)]
SIDES = [d for d in itertools.product((-1, 0, 1), repeat=2) if d != (0, 0)]
TILES = [d for d in NEAR if d[0] == 0]
LINES = [d for d in NEAR if d[0] != 0]
LAST_SIDES = [(-1, 0), (-1, -1), (0, -1)]
LAST_TILES = [(0, 0, -1), (0, -1, -1)]
LAST_LINES = [(-1, 0, -1), (-1, -1, -1)]


def span(step):
    return {1: (slice(4, 5), slice(0, 1)), -1: (slice(1, 2), slice(5, 6)), 0: (slice(1, 5), slice(1, 5))}[step]


def rows_of(step):
    return {1: (slice(39, 40), slice(7, 8)), -1: (slice(8, 9), slice(40, 41)), 0: (slice(8, 40), slice(8, 40))}[step]


def kernel(sizes, disp, dens, mat, fix, adj_out, sens_out, sum_out, *scratch):
    (U, FI, AD, DN, MT, FX, PS, QS, R6, KF, S0, SE, FD, TS, LS, TR, LR, PL, PK, WP, SUM, in_sem,
     f1s, f1r, t1s, t1r, l1s, l1r, f2s, f2r, t2s, t2r, l2s, l2r, f3s, f3r, t3s, t3r, l3s, l3r, ass, asr) = scratch
    nx, ny, nz = sizes
    me = (lax.axis_index("gx"), lax.axis_index("gy"), lax.axis_index("gz"))
    lane = lax.broadcasted_iota(jnp.int32, (8, 128), 1)
    sub = lax.broadcasted_iota(jnp.int32, (8, 128), 0)
    first_lane = lane == 0
    last_lane = lane == 127

    def exists(step):
        ok = None
        for i, s, n in zip(me, step, sizes):
            if s:
                one = i < n - 1 if s > 0 else i > 0
                ok = one if ok is None else jnp.logical_and(ok, one)
        return ok

    def at(step):
        return tuple(i + s for i, s in zip(me, step))

    def back(step):
        return tuple(-s for s in step)

    barrier = pltpu.get_barrier_semaphore()

    def greet(device):
        pl.semaphore_signal(barrier, inc=1, device_id=device, device_id_type=MESH)

    rings = []
    for axis, n in enumerate(sizes):
        for k in range(1, n):
            peer = list(me)
            peer[axis] = lax.rem(me[axis] + k, n)
            rings.append((axis, k, tuple(peer)))
            greet(tuple(peer))
    for step in NEAR:
        pl.when(exists(step))(functools.partial(greet, at(step)))

    loads = []
    for lt in range(2):
        cols = pl.ds(lt * 128, 128)
        loads.append(pltpu.make_async_copy(disp.at[:, :, :, cols], U.at[0:3, 1:5, lt, 8:40, :], in_sem.at[4 * lt]))
        loads.append(pltpu.make_async_copy(dens.at[:, :, cols], DN.at[:, lt], in_sem.at[4 * lt + 1]))
        loads.append(pltpu.make_async_copy(mat.at[:, :, cols], MT.at[:, lt], in_sem.at[4 * lt + 2]))
        loads.append(pltpu.make_async_copy(fix.at[:, :, cols], FX.at[:, lt], in_sem.at[4 * lt + 3]))
    for c in loads:
        c.start()

    def plane_of(step):
        return 1 - step[2]

    def clear(k, ref, comps):
        for step, where in (((-1, 0, 0), 0), ((1, 0, 0), 5)):
            def fill(where=where):
                for c in range(comps):
                    for lt in range(2):
                        ref[c, where, lt, 7:41, :] = jnp.full((34, 128), -1.0 if c == 3 else 0.0, F32)
            pl.when(jnp.logical_not(exists(step)))(fill)
        for step, row in (((0, -1, 0), 7), ((0, 1, 0), 40)):
            def fill(row=row):
                for c in range(comps):
                    for x in range(6):
                        for lt in range(2):
                            ref[c, x, lt, row : row + 1, :] = jnp.full((1, 128), -1.0 if c == 3 else 0.0, F32)
            pl.when(jnp.logical_not(exists(step)))(fill)
        outside = jnp.where(lane % 4 == 3, -1.0, 0.0)
        for step in TILES:
            def fill(step=step):
                TR[k, plane_of(step), step[1] + 1] = outside
            pl.when(jnp.logical_not(exists(back(step))))(fill)
        for step in LINES:
            def fill(step=step):
                LR[k, plane_of(step), (step[0] + 1) // 2, step[1] + 1] = outside[0:1]
            pl.when(jnp.logical_not(exists(back(step))))(fill)

    clear(0, U, 4)
    clear(1, FI, 3)
    clear(2, AD, 3)
    for c in loads:
        c.wait()

    for x in range(4):
        for lt in range(2):
            m = MT[x, lt]
            U[3, x + 1, lt, 8:40, :] = jnp.where(m == 1, DN[x, lt], jnp.where(m == 2, 1.0, 0.0))

    def pack(ref, comps, high, xs):
        lt, source = (1, 127) if high else (0, 0)
        parts = []
        for g in range(4):
            part = jnp.zeros((8, 128), F32)
            for c in range(comps):
                for x in xs:
                    to = 32 * g + 4 * x + c
                    v = ref[c, x, lt, 8 + 8 * g : 16 + 8 * g, :]
                    part = jnp.where(lane == to, pltpu.roll(v, (to - source) % 128, 1), part)
            parts.append(part)
        return (parts[0] + parts[1]) + (parts[2] + parts[3])

    def line(tile, x):
        out = jnp.zeros((8, 128), F32)
        mine = (lane % 32) // 4 == 7 - sub
        for i in range(8):
            out = jnp.where(jnp.logical_and(mine, sub == i), pltpu.roll(tile, (28 - 4 * i - 4 * x) % 128, 1), out)
        return jnp.sum(out, axis=0, keepdims=True)

    def spread(row, x):
        moved = pltpu.roll(jnp.broadcast_to(row, (8, 128)), 0, 1, stride=4, stride_axis=0)
        return pltpu.roll(moved, (100 + 4 * x) % 128, 1)

    def remote(src, dst, send, recv, step):
        return (step, pltpu.make_async_remote_copy(
            src_ref=src, dst_ref=dst, send_sem=send, recv_sem=recv, device_id=at(step), device_id_type=MESH))

    def sides(ref, steps, comps_of, send, recv):
        out = []
        for i, (dx, dy) in enumerate(steps):
            (sx, tx), (sr, tr) = span(dx), rows_of(dy)
            comps = slice(0, comps_of(dx, dy))
            out.append(remote(ref.at[comps, sx, :, sr, :], ref.at[comps, tx, :, tr, :], send.at[i], recv.at[i], (dx, dy, 0)))
        return out

    def tiles(k, steps, send, recv):
        return [remote(TS.at[k, 1 if step[2] > 0 else 0], TR.at[k, plane_of(step), step[1] + 1], send.at[i], recv.at[i], step)
                for i, step in enumerate(steps)]

    def lines(k, steps, send, recv):
        return [remote(LS.at[k, 1 if step[2] > 0 else 0, (step[0] + 1) // 2],
                       LR.at[k, plane_of(step), (step[0] + 1) // 2, step[1] + 1], send.at[i], recv.at[i], step)
                for i, step in enumerate(steps)]

    def along(copies):
        return [c for c in copies if c[0][0] == 0], [c for c in copies if c[0][0] != 0]

    def start(copies):
        for step, c in copies:
            pl.when(exists(step))(c.start)

    def arrive(copies):
        for step, c in copies:
            pl.when(exists(back(step)))(c.wait_recv)

    def left(copies):
        for step, c in copies:
            pl.when(exists(step))(c.wait_send)

    def merge(k, plane, with_x):
        for dy in (-1, 0, 1):
            full = TS[k, 0] if plane == 1 and dy == 0 else TR[k, plane, dy + 1]
            if with_x:
                full = jnp.where(lane % 32 < 4, spread(LR[k, plane, 1, dy + 1], 0), full)
                full = jnp.where(lane % 32 >= 20, spread(LR[k, plane, 0, dy + 1], 5), full)
            if dy == 0:
                for g in range(4):
                    PL[plane, 8 + 8 * g : 16 + 8 * g, :] = pltpu.roll(full, (128 - 32 * g) % 128, 1) if g else full
            elif dy == 1:
                PL[plane, 0:8, :] = pltpu.roll(full, 32, 1)
            else:
                PL[plane, 40:48, :] = full

    def sweep_z(ref, xs):
        def body(g, carry):
            rows = pl.ds(7 + 8 * g, 8)
            edge = PL[2, rows, :]
            for c in range(3):
                for x in xs:
                    t0, t1 = ref[c, x, 0, rows, :], ref[c, x, 1, rows, :]
                    r0, r1 = pltpu.roll(t0, 127, 1), pltpu.roll(t1, 127, 1)
                    s0 = jnp.where(last_lane, r1, r0)
                    s1 = jnp.where(last_lane, pltpu.roll(edge, 127 - 4 * x - c, 1), r1)
                    PS[c, x, 0, rows, :] = s0 + t0
                    PS[c, x, 1, rows, :] = s1 + t1
                    QS[c, x, 0, rows, :] = s0 - t0
                    QS[c, x, 1, rows, :] = s1 - t1
            return carry
        lax.fori_loop(0, 5, body, 0)

    def gradients(low, high):
        return [[high[c][0] - low[c][0] for c in range(3)], [high[c][1] + low[c][1] for c in range(3)],
                [high[c][2] + low[c][2] for c in range(3)]]

    def strain6(g):
        gx, gy, gz = g
        return gx[0], gy[1], gz[2], gy[0] + gx[1], gz[1] + gy[2], gx[2] + gz[0]

    def y_sums(x, lt, base):
        out = []
        for c in range(3):
            p0, p1 = PS[c, x, lt, pl.ds(base, 8), :], PS[c, x, lt, pl.ds(base + 1, 8), :]
            q0, q1 = QS[c, x, lt, pl.ds(base, 8), :], QS[c, x, lt, pl.ds(base + 1, 8), :]
            out.append((p0 + p1, p1 - p0, q0 + q1))
        return out

    def packed_strain():
        lo, hi = PL[0], PL[1]
        PK[0] = lo + hi
        PK[1] = hi - lo
        p0, p1, q0, q1 = PK[0, 0:40], PK[0, 1:41], PK[1, 0:40], PK[1, 1:41]
        a, b, c = p0 + p1, p1 - p0, q0 + q1
        g = [pltpu.roll(a, 124, 1) - a, pltpu.roll(b, 124, 1) + b, pltpu.roll(c, 124, 1) + c]
        return strain6([[t] + [pltpu.roll(t, 128 - i, 1) for i in (1, 2)] for t in g])

    def stiffness(d):
        return jnp.where(d < 0.0, 0.0, 0.001 + d * d * d)

    def load_terms(e, d):
        a, b, c = e[0] - e[1], e[1] - e[2], e[2] - e[0]
        q = (MU * MU / 16.0) * (2.0 * (a * a + b * b + c * c) + 3.0 * (e[3] * e[3] + e[4] * e[4] + e[5] * e[5]))
        vm = d * q
        w = vm * vm * vm
        t = (-MU * MU / 8.0 * BOOST) * (w * d)
        ts = 1.5 * t
        return q, vm, w, (t * (a - c), t * (b - a), t * (c - b), ts * e[3], ts * e[4], ts * e[5])

    def stiff_terms(e, kf):
        k = kf * (-2.0 * MU / 16.0)
        tr = (kf * (-LAM / 16.0)) * (e[0] + e[1] + e[2])
        ks = kf * (-MU / 16.0)
        return tr + k * e[0], tr + k * e[1], tr + k * e[2], ks * e[3], ks * e[4], ks * e[5]

    S_Y, D_Y = (0, 3, 5, 4, 2), (3, 1, 4)

    def x_parts(low, high):
        (sl, dl), (sh, dh) = low, high
        return [((sh[i] - sl[i]) + (dh[j] + dl[j]), sh[k] + sl[k]) for i, j, k in ((0, 3, 5), (3, 1, 4), (5, 4, 2))]

    def packed_forces(r):
        for i in range(6):
            PK[i, 0:40] = r[i]
        s = {i: PK[i, 7:39] + PK[i, 8:40] for i in S_Y}
        d = {i: PK[i, 8:40] - PK[i, 7:39] for i in D_Y}
        high = ({i: pltpu.roll(v, 124, 1) for i, v in s.items()}, {i: pltpu.roll(v, 124, 1) for i, v in d.items()})
        for c, (u, w) in enumerate(x_parts((s, d), high)):
            WP[c] = u - w

    def from_low(w0, w1, packed, x):
        r0, r1 = pltpu.roll(w0, 1, 1), pltpu.roll(w1, 1, 1)
        edge = pltpu.roll(packed, 128 - 4 * x, 1) if x else packed
        return jnp.where(first_lane, edge, r0), jnp.where(first_lane, r0, r1)

    def forces(xs, finish):
        def body(g, carry):
            base = pl.multiple_of(8 + 8 * g, 8)
            own = pl.ds(pl.multiple_of(8 * g, 8), 8)
            packed = [WP[c, own, :] for c in range(3)]

            def sums(x):
                out = []
                for lt in range(2):
                    r1 = [R6[i, x, lt, pl.ds(base, 8), :] for i in range(6)]
                    r0 = [R6[i, x, lt, pl.ds(base - 1, 8), :] for i in range(6)]
                    out.append(({i: r0[i] + r1[i] for i in S_Y}, {i: r1[i] - r0[i] for i in D_Y}))
                return out

            low = sums(xs[0])
            for x in xs:
                high = sums(x + 1)
                p0, p1 = x_parts(low[0], high[0]), x_parts(low[1], high[1])
                for c in range(3):
                    (u0, c0), (u1, c1) = p0[c], p1[c]
                    s0, s1 = from_low(u0 - c0, u1 - c1, packed[c], x)
                    finish(c, x, 0, base, own, u0 + c0 + s0)
                    finish(c, x, 1, base, own, u1 + c1 + s1)
                low = high
            return carry
        lax.fori_loop(0, 4, body, 0)

    def send_tiles(k, ref, comps, copies):
        TS[k, 0] = pack(ref, comps, False, range(1, 5))
        TS[k, 1] = pack(ref, comps, True, range(1, 5))
        start(copies)

    def put_lines(k, low, high):
        for z, t in enumerate((low, high)):
            LS[k, z, 0] = line(t, 1)
            LS[k, z, 1] = line(t, 4)

    TS[0, 0] = pack(U, 4, False, range(1, 5))
    TS[0, 1] = pack(U, 4, True, range(1, 5))
    put_lines(0, TS[0, 0], TS[0, 1])

    t1 = tiles(0, TILES, t1s, t1r)
    l1 = lines(0, LINES, l1s, l1r)
    f1, x1 = along(sides(U, SIDES, lambda dx, dy: 4 if dx >= 0 and dy >= 0 else 3, f1s, f1r))
    t2 = tiles(1, TILES, t2s, t2r)
    l2 = lines(1, LINES, l2s, l2r)
    f2, x2 = along(sides(FI, SIDES, lambda dx, dy: 3, f2s, f2r))
    t3 = tiles(2, LAST_TILES, t3s, t3r)
    l3 = lines(2, LAST_LINES, l3s, l3r)
    f3, x3 = along(sides(AD, LAST_SIDES, lambda dx, dy: 3, f3s, f3r))

    block = 1
    for i, n in zip(me, sizes):
        block = block * (1 + (i > 0).astype(jnp.int32) + (i < n - 1).astype(jnp.int32))
    pl.semaphore_wait(barrier, block - 1 + len(rings))

    start(l1)
    start(x1)
    start(t1)
    start(f1)

    def power(xs, total):
        def body(g, total):
            base = pl.multiple_of(8 * g, 8)
            rows = pl.ds(base, 8)
            own = pl.ds(pl.multiple_of(jnp.maximum(8 * g - 8, 0), 8), 8)
            inside = jnp.full((8, 128), g, jnp.int32) > 0
            for lt in range(2):
                low = y_sums(xs[0], lt, base)
                for x in xs:
                    high = y_sums(x + 1, lt, base)
                    e = strain6(gradients(low, high))
                    low = high
                    q, vm, w, r = load_terms(e, jnp.maximum(U[3, x, lt, rows, :], 0.0))
                    for i in range(6):
                        R6[i, x, lt, rows, :] = r[i]
                    if x > 0:
                        v2 = vm * vm
                        total = total + jnp.where(inside, v2 * v2, 0.0)
                        tr = (LAM / 16.0) * (e[0] + e[1] + e[2])
                        for i in range(6):
                            S0[i, x - 1, lt, own, :] = tr + (MU / 8.0) * e[i] if i < 3 else (MU / 16.0) * e[i]
                        SE[x - 1, lt, own, :] = jnp.where(MT[x - 1, lt, own, :] == 1, (0.5 * BOOST) * (w * q), 0.0)
            return total
        return lax.fori_loop(0, 5, body, total)

    def fill_stiffness(xs):
        for x in xs:
            for lt in range(2):
                KF[x, lt, 0:40, :] = stiffness(U[3, x, lt, 0:40, :])

    def packed_load():
        d = pltpu.roll(PL[0, 0:40, :], 125, 1)
        kp = stiffness(d)
        packed_forces(load_terms(packed_strain(), jnp.maximum(d, 0.0))[3])
        PK[6, 0:40] = kp
        ky = PK[6, 7:39] + PK[6, 8:40]
        WP[3] = ky + pltpu.roll(ky, 124, 1)

    def diagonal(xs):
        def body(g, carry):
            base = pl.multiple_of(8 + 8 * g, 8)
            own = pl.ds(pl.multiple_of(8 * g, 8), 8)
            packed = WP[3, own, :]

            def sums(x):
                return [KF[x, lt, pl.ds(base, 8), :] + KF[x, lt, pl.ds(base - 1, 8), :] for lt in range(2)]

            low = sums(xs[0])
            for x in xs:
                high = sums(x + 1)
                k0, k1 = low[0] + high[0], low[1] + high[1]
                s0, s1 = from_low(k0, k1, packed, x)
                for lt, k in ((0, k0 + s0), (1, k1 + s1)):
                    fixed = FX[x, lt, own, :].astype(F32)
                    FD[x, lt, own, :] = (1.0 - fixed) / (DIAG * k + fixed)
                low = high
            return carry
        lax.fori_loop(0, 4, body, 0)

    def first_out(c, x, lt, base, own, value):
        FI[c, x + 1, lt, pl.ds(base, 8), :] = value * FD[x, lt, own, :]

    arrive(t1)
    arrive(f1)
    for plane in range(3):
        merge(0, plane, False)
    packed_load()
    sweep_z(U, range(1, 5))
    total = power((1, 2, 3), jnp.zeros((8, 128), F32))
    fill_stiffness(range(1, 5))
    diagonal((1, 2, 3))
    forces((1, 2), first_out)

    arrive(l1)
    arrive(x1)
    for plane in range(3):
        merge(0, plane, True)
    packed_load()
    sweep_z(U, (0, 5))
    fill_stiffness((0,))
    diagonal((0,))
    power((0,), total)
    total = power((4,), total)
    forces((0,), first_out)
    forces((3,), first_out)
    start(x2)
    TS[1, 0] = pack(FI, 3, False, range(1, 5))
    TS[1, 1] = pack(FI, 3, True, range(1, 5))
    put_lines(1, TS[1, 0], TS[1, 1])
    start(l2)
    start(t2)
    start(f2)

    order = (2, 1, 0)

    def ring(stage):
        axis, out = order[stage], []
        for i, (a, k, peer) in enumerate(rings):
            if a == axis:
                out.append(pltpu.make_async_remote_copy(
                    src_ref=SUM.at[stage, me[axis]], dst_ref=SUM.at[stage, me[axis]],
                    send_sem=ass.at[i], recv_sem=asr.at[i], device_id=peer, device_id_type=MESH))
        return out

    def send_sum(stage, value):
        SUM[stage, me[order[stage]]] = value
        for c in ring(stage):
            c.start()

    def take_sum(stage):
        for c in ring(stage):
            c.wait_recv()
        value = SUM[stage, 0]
        for i in range(1, sizes[order[stage]]):
            value = value + SUM[stage, i]
        return value

    send_sum(0, total)

    def stiff(xs):
        def body(g, carry):
            base = pl.multiple_of(8 * g, 8)
            rows = pl.ds(base, 8)
            for lt in range(2):
                low = y_sums(xs[0], lt, base)
                for x in xs:
                    high = y_sums(x + 1, lt, base)
                    r = stiff_terms(strain6(gradients(low, high)), KF[x, lt, rows, :])
                    low = high
                    for i in range(6):
                        R6[i, x, lt, rows, :] = r[i]
            return carry
        lax.fori_loop(0, 5, body, 0)

    def packed_stiff():
        packed_forces(stiff_terms(packed_strain(), kp_ref[...]))

    def adjoint_out(c, x, lt, base, own, value):
        new = (1.0 + RELAX) * FI[c, x + 1, lt, pl.ds(base, 8), :] - RELAX * FD[x, lt, own, :] * value
        AD[c, x + 1, lt, pl.ds(base, 8), :] = new
        adj_out[c, x, lt, own, :] = new

    kp_ref = PK.at[6, 0:40]
    arrive(t2)
    arrive(f2)
    for plane in range(3):
        merge(1, plane, False)
    packed_stiff()
    sweep_z(FI, range(1, 5))
    stiff((1, 2, 3))
    forces((1, 2), adjoint_out)
    send_sum(1, take_sum(0))
    arrive(l2)
    arrive(x2)
    for plane in range(3):
        merge(1, plane, True)
    packed_stiff()
    sweep_z(FI, (0, 5))
    stiff((0,))
    forces((0,), adjoint_out)
    start(x3)
    edge = pack(AD, 3, False, (1,))
    LS[2, 0, 0] = line(edge, 1)
    start(l3)
    stiff((4,))
    forces((3,), adjoint_out)
    TS[2, 0] = edge + pack(AD, 3, False, (2, 3, 4))
    start(t3)
    start(f3)
    send_sum(2, take_sum(1))

    def last(xs):
        def body(g, carry):
            base = pl.multiple_of(8 + 8 * g, 8)
            rows = pl.ds(base, 8)
            own = pl.ds(pl.multiple_of(8 * g, 8), 8)
            for lt in range(2):
                low = y_sums(xs[0] + 1, lt, base)
                for x in xs:
                    high = y_sums(x + 2, lt, base)
                    e = strain6(gradients(low, high))
                    low = high
                    dot = e[0] * S0[0, x, lt, own, :]
                    for i in range(1, 6):
                        dot = dot + e[i] * S0[i, x, lt, own, :]
                    d = U[3, x + 1, lt, rows, :]
                    slope = jnp.where(MT[x, lt, own, :] == 1, 3.0 * (d * d), 0.0)
                    sens_out[x, lt, own, :] = SE[x, lt, own, :] - slope * dot
            return carry
        lax.fori_loop(0, 4, body, 0)

    arrive(t3)
    arrive(f3)
    merge(2, 2, False)
    sweep_z(AD, range(1, 5))
    last((0, 1, 2))
    arrive(l3)
    arrive(x3)
    merge(2, 2, True)
    sweep_z(AD, (5,))
    last((3,))
    sum_out[...] = take_sum(2)
    for copies in (t1, l1, f1, x1, t2, l2, f2, x2, t3, l3, f3, x3):
        left(copies)
    for stage in range(3):
        for c in ring(stage):
            c.wait_send()


def finish_kernel(count, adj, sens, total, adj_out, sens_out):
    mean = jnp.full((8, 128), jnp.sum(total[...]) * (1.0 / count) + SHIFT, F32)
    scale = (jnp.sqrt(jnp.sqrt(jnp.sqrt(mean))) / mean * (1.0 / BOOST))[0:1]
    for x in range(4):
        for lt in range(2):
            cols = slice(128 * lt, 128 * lt + 128)
            sens_out[x, :, cols] = sens[x, lt] * scale
            for c in range(3):
                adj_out[c, x, :, cols] = adj[c, x, lt] * scale


def solution(mesh):
    sizes = tuple(mesh.shape[a] for a in ("gx", "gy", "gz"))
    peers = sum(sizes) - 3
    count = sizes[0] * sizes[1] * sizes[2] * 4 * 32 * 256

    def per_device(displacement, density, material, fixed_mask):
        dma = pltpu.SemaphoreType.DMA
        vmem = pl.BlockSpec(memory_space=pltpu.VMEM)
        both = lambda n: [dma((n,)), dma((n,))]
        adj, sens, total = pl.pallas_call(
            functools.partial(kernel, sizes),
            out_shape=(jax.ShapeDtypeStruct((3, 4, 2, 32, 128), F32), jax.ShapeDtypeStruct((4, 2, 32, 128), F32),
                       jax.ShapeDtypeStruct((8, 128), F32)),
            in_specs=[pl.BlockSpec(memory_space=pl.ANY)] * 4,
            out_specs=[vmem] * 3,
            scratch_shapes=[
                pltpu.VMEM((4, 6, 2, ROWS, 128), F32),
                pltpu.VMEM((3, 6, 2, ROWS, 128), F32),
                pltpu.VMEM((3, 6, 2, ROWS, 128), F32),
                pltpu.VMEM((4, 2, 32, 128), F32),
                pltpu.VMEM((4, 2, 32, 128), jnp.int32),
                pltpu.VMEM((4, 2, 32, 128), jnp.int32),
                pltpu.VMEM((3, 6, 2, ROWS, 128), F32),
                pltpu.VMEM((3, 6, 2, ROWS, 128), F32),
                pltpu.VMEM((6, 5, 2, ROWS, 128), F32),
                pltpu.VMEM((5, 2, ROWS, 128), F32),
                pltpu.VMEM((6, 4, 2, 32, 128), F32),
                pltpu.VMEM((4, 2, 32, 128), F32),
                pltpu.VMEM((4, 2, 32, 128), F32),
                pltpu.VMEM((3, 2, 8, 128), F32),
                pltpu.VMEM((3, 2, 2, 1, 128), F32),
                pltpu.VMEM((3, 3, 3, 8, 128), F32),
                pltpu.VMEM((3, 3, 2, 3, 1, 128), F32),
                pltpu.VMEM((3, ROWS, 128), F32),
                pltpu.VMEM((7, ROWS, 128), F32),
                pltpu.VMEM((4, 32, 128), F32),
                pltpu.VMEM((3, 8, 8, 128), F32),
                dma((8,)),
                *both(8), *both(8), *both(18),
                *both(8), *both(8), *both(18),
                *both(3), *both(2), *both(2),
                *both(peers),
            ],
            compiler_params=pltpu.CompilerParams(collective_id=0, has_side_effects=True),
        )(displacement, density, material, fixed_mask)
        return pl.pallas_call(
            functools.partial(finish_kernel, count),
            out_shape=(jax.ShapeDtypeStruct((3, 4, 32, 256), F32), jax.ShapeDtypeStruct((4, 32, 256), F32)),
            in_specs=[vmem] * 3,
            out_specs=[vmem] * 2,
        )(adj, sens, total)

    placed = (P(None, "gx", "gy", "gz"), P("gx", "gy", "gz"), P("gx", "gy", "gz"), P("gx", "gy", "gz"))
    return jax.shard_map(per_device, mesh=mesh, in_specs=placed, out_specs=(placed[0], placed[1]), check_vma=False)
```

time: 47.6 us -> 44.9 us (0.943)
  the two profiles are of different devices: /device:TPU:57 before, /device:TPU:1 now
where the time goes in v2:
time: 44.9 us; the launch traced here: 44.6 us
  Pallas kernels  44 us (98%)
  between operations  0.64 us (1%)
    pallas_call x1, Pallas kernels, per_device(): pl.pallas_call(functools.partial(kernel, sizes), out_shape=(jax.ShapeDtyp...  42 us
    pallas_call x1, Pallas kernels, per_device(): pl.pallas_call(functools.partial(finish_kernel, count), out_shape=(jax.Sh...  2.03 us

profile of v2, /device:TPU:1, one launch (start us, length us, event | category | flops | bytes accessed | tf_op | source)
XLA Modules:
  0.0 44.6 jit_solution(10674991039492108049)
XLA Ops:
  0.6 42.0 %shard_map.59 = (f32[3,4,2,32,128]{4,3,2,1,0:T(8,128)}, f32[4,2,32,128]{3,2,1,0:T(8,128)}, f32[8,128]{1,0:T(8,128)}) custom-call(f32[3,4,32,256]{3,2,1,0:T(8,128)} %disp.1, f32[4,32,256]{2,1,0:T(8,128)} %dens.1, s32[4,32,256]{2,1,0:T(8,128)} %mat.1, s32[4,32,256]{2,1,0:T(8,128)} %fix.1), custom_call_target="tpu_custom_call" | custom-call | tf_op jit(solution)/shard_map/pallas_call | solution.py:568
  42.6 2.0 %shard_map.60 = (f32[3,4,32,256]{3,2,1,0:T(8,128)}, f32[4,32,256]{2,1,0:T(8,128)}) custom-call(f32[3,4,2,32,128]{4,3,2,1,0:T(8,128)} %get-tuple-element.5.adj, f32[4,2,32,128]{3,2,1,0:T(8,128)} %get-tuple-element.6.sens, f32[8,128]{1,0:T(8,128)} %get-tuple-element.7.total), custom_call_target="tpu_custom_call" | custom-call | tf_op jit(solution)/shard_map/pallas_call | solution.py:604

commit v3 on v2

--- a/solution.py
+++ b/solution.py
@@ -15,19 +15,20 @@
 SHIFT = 1e-06
 BOOST = 2.0**18
 MESH = pl.DeviceIdType.MESH
+ROUTE = (0, 1, 2)
+ORDER = (0, 1, 2)
 F32 = jnp.float32
 ROWS = 48
 NEAR = [d for d in itertools.product((-1, 0, 1), repeat=3) if d != (0, 0, 0)]
 SIDES = [d for d in itertools.product((-1, 0, 1), repeat=2) if d != (0, 0)]
 TILES = [d for d in NEAR if d[0] == 0]
 LINES = [d for d in NEAR if d[0] != 0]
-LAST_SIDES = [(-1, 0), (-1, -1), (0, -1)]
 LAST_TILES = [(0, 0, -1), (0, -1, -1)]
-LAST_LINES = [(-1, 0, -1), (-1, -1, -1)]
+OUTSIDE = (0.0, 0.0, 0.0, -1.0, 1.0)
 
 
 def span(step):
-    return {1: (slice(4, 5), slice(0, 1)), -1: (slice(1, 2), slice(5, 6)), 0: (slice(1, 5), slice(1, 5))}[step]
+    return {1: (slice(4, 6), slice(0, 2)), -1: (slice(2, 5), slice(6, 9)), 0: (slice(2, 6), slice(2, 6))}[step]
 
 
 def rows_of(step):
@@ -35,8 +36,8 @@
 
 
 def kernel(sizes, disp, dens, mat, fix, adj_out, sens_out, sum_out, *scratch):
-    (U, FI, AD, DN, MT, FX, PS, QS, R6, KF, S0, SE, FD, TS, LS, TR, LR, PL, PK, WP, SUM, in_sem,
-     f1s, f1r, t1s, t1r, l1s, l1r, f2s, f2r, t2s, t2r, l2s, l2r, f3s, f3r, t3s, t3r, l3s, l3r, ass, asr) = scratch
+    (U, FI, AD, DN, MT, FX, PS, QS, R6, KF, S0, SE, FD, TS, LS, TR, LR, PL, PK, WP, SUM, SUM2, ST, in_sem,
+     xs_, xr_, hs_, hr_, f1s, f1r, t1s, t1r, l1s, l1r, f2s, f2r, t2s, t2r, f3s, f3r, t3s, t3r, ass, asr) = scratch
     nx, ny, nz = sizes
     me = (lax.axis_index("gx"), lax.axis_index("gy"), lax.axis_index("gz"))
     lane = lax.broadcasted_iota(jnp.int32, (8, 128), 1)
@@ -63,20 +64,22 @@
     def greet(device):
         pl.semaphore_signal(barrier, inc=1, device_id=device, device_id_type=MESH)
 
+    place = (me[2], me[0] * ny + me[1])
     rings = []
-    for axis, n in enumerate(sizes):
-        for k in range(1, n):
-            peer = list(me)
-            peer[axis] = lax.rem(me[axis] + k, n)
-            rings.append((axis, k, tuple(peer)))
-            greet(tuple(peer))
+    for k in range(1, nz):
+        rings.append((0, (me[0], me[1], lax.rem(me[2] + k, nz))))
+    for k in range(1, nx * ny):
+        other = lax.rem(place[1] + k, nx * ny)
+        rings.append((1, (other // ny, lax.rem(other, ny), me[2])))
+    for _, peer in rings:
+        greet(peer)
     for step in NEAR:
         pl.when(exists(step))(functools.partial(greet, at(step)))
 
     loads = []
     for lt in range(2):
         cols = pl.ds(lt * 128, 128)
-        loads.append(pltpu.make_async_copy(disp.at[:, :, :, cols], U.at[0:3, 1:5, lt, 8:40, :], in_sem.at[4 * lt]))
+        loads.append(pltpu.make_async_copy(disp.at[:, :, :, cols], U.at[0:3, 2:6, lt, 8:40, :], in_sem.at[4 * lt]))
         loads.append(pltpu.make_async_copy(dens.at[:, :, cols], DN.at[:, lt], in_sem.at[4 * lt + 1]))
         loads.append(pltpu.make_async_copy(mat.at[:, :, cols], MT.at[:, lt], in_sem.at[4 * lt + 2]))
         loads.append(pltpu.make_async_copy(fix.at[:, :, cols], FX.at[:, lt], in_sem.at[4 * lt + 3]))
@@ -87,29 +90,31 @@
         return 1 - step[2]
 
     def clear(k, ref, comps):
-        for step, where in (((-1, 0, 0), 0), ((1, 0, 0), 5)):
-            def fill(where=where):
-                for c in range(comps):
-                    for lt in range(2):
-                        ref[c, where, lt, 7:41, :] = jnp.full((34, 128), -1.0 if c == 3 else 0.0, F32)
-            pl.when(jnp.logical_not(exists(step)))(fill)
         for step, row in (((0, -1, 0), 7), ((0, 1, 0), 40)):
             def fill(row=row):
                 for c in range(comps):
-                    for x in range(6):
+                    for x in range(9):
                         for lt in range(2):
-                            ref[c, x, lt, row : row + 1, :] = jnp.full((1, 128), -1.0 if c == 3 else 0.0, F32)
+                            ref[c, x, lt, row : row + 1, :] = jnp.full((1, 128), OUTSIDE[c], F32)
             pl.when(jnp.logical_not(exists(step)))(fill)
-        outside = jnp.where(lane % 4 == 3, -1.0, 0.0)
         for step in TILES:
             def fill(step=step):
                 TR[k, plane_of(step), step[1] + 1] = outside
             pl.when(jnp.logical_not(exists(back(step))))(fill)
-        for step in LINES:
-            def fill(step=step):
-                LR[k, plane_of(step), (step[0] + 1) // 2, step[1] + 1] = outside[0:1]
-            pl.when(jnp.logical_not(exists(back(step))))(fill)
-
+
+    outside = jnp.where(lane % 4 == 3, -1.0, 0.0)
+    for step, planes in (((-1, 0, 0), (0, 1)), ((1, 0, 0), (6, 7, 8))):
+        def fill(planes=planes):
+            for c in range(5):
+                for x in planes:
+                    for lt in range(2):
+                        U[c, x, lt, 7:41, :] = jnp.full((34, 128), OUTSIDE[c], F32)
+        pl.when(jnp.logical_not(exists(step)))(fill)
+    for step in LINES:
+        def fill(step=step):
+            for i in range(3):
+                LR[plane_of(step), (1 - step[0]) // 2, step[1] + 1, i] = outside[0:1]
+        pl.when(jnp.logical_not(exists(back(step))))(fill)
     clear(0, U, 4)
     clear(1, FI, 3)
     clear(2, AD, 3)
@@ -119,7 +124,8 @@
     for x in range(4):
         for lt in range(2):
             m = MT[x, lt]
-            U[3, x + 1, lt, 8:40, :] = jnp.where(m == 1, DN[x, lt], jnp.where(m == 2, 1.0, 0.0))
+            U[3, x + 2, lt, 8:40, :] = jnp.where(m == 1, DN[x, lt], jnp.where(m == 2, 1.0, 0.0))
+            U[4, x + 2, lt, 8:40, :] = FX[x, lt].astype(F32)
 
     def pack(ref, comps, high, xs):
         lt, source = (1, 127) if high else (0, 0)
@@ -149,22 +155,89 @@
         return (step, pltpu.make_async_remote_copy(
             src_ref=src, dst_ref=dst, send_sem=send, recv_sem=recv, device_id=at(step), device_id_type=MESH))
 
-    def sides(ref, steps, comps_of, send, recv):
+    def sides(ref, steps, comps, planes, send, recv):
         out = []
         for i, (dx, dy) in enumerate(steps):
-            (sx, tx), (sr, tr) = span(dx), rows_of(dy)
-            comps = slice(0, comps_of(dx, dy))
-            out.append(remote(ref.at[comps, sx, :, sr, :], ref.at[comps, tx, :, tr, :], send.at[i], recv.at[i], (dx, dy, 0)))
+            (sx, tx), (sr, tr) = span(dx) if dx else (planes, planes), rows_of(dy)
+            out.append(remote(ref.at[0:comps, sx, :, sr, :], ref.at[0:comps, tx, :, tr, :], send.at[i], recv.at[i], (dx, dy, 0)))
         return out
 
     def tiles(k, steps, send, recv):
         return [remote(TS.at[k, 1 if step[2] > 0 else 0], TR.at[k, plane_of(step), step[1] + 1], send.at[i], recv.at[i], step)
                 for i, step in enumerate(steps)]
 
-    def lines(k, steps, send, recv):
-        return [remote(LS.at[k, 1 if step[2] > 0 else 0, (step[0] + 1) // 2],
-                       LR.at[k, plane_of(step), (step[0] + 1) // 2, step[1] + 1], send.at[i], recv.at[i], step)
-                for i, step in enumerate(steps)]
+    def lines(steps, send, recv):
+        out = []
+        for i, step in enumerate(steps):
+            planes, count, side = (slice(2, 4), 2, 0) if step[0] > 0 else (slice(0, 3), 3, 1)
+            out.append(remote(LS.at[1 if step[2] > 0 else 0, planes], LR.at[plane_of(step), side, step[1] + 1, 0:count],
+                              send.at[i], recv.at[i], step))
+        return out
+
+    middle = nx // 2
+    own = slice(8, 40)
+
+    def plane_copy(comps, src, dst, i, step):
+        return remote(U.at[comps, src, :, own, :], U.at[comps, dst, :, own, :], xs_.at[i], xr_.at[i], step)
+
+    wide = [plane_copy(slice(0, 3), slice(4, 6), slice(0, 2), 0, (1, 0, 0)), plane_copy(slice(0, 3), slice(2, 5), slice(6, 9), 1, (-1, 0, 0))]
+    thin = [plane_copy(slice(3, 5), slice(4, 6), slice(0, 2), 2, (1, 0, 0)), plane_copy(slice(3, 5), slice(2, 4), slice(6, 8), 3, (-1, 0, 0))]
+    low_side, high_side = me[0] == middle - 1, me[0] == middle
+
+    def plain(step):
+        return jnp.logical_and(exists(step), jnp.logical_not(low_side if step[0] > 0 else high_side))
+
+    def hop(c, up, leg):
+        count = 2 if up else 3
+        src = U.at[c, slice(4, 6) if up else slice(2, 5), :, own, :]
+        dst = U.at[c, slice(0, 2) if up else slice(6, 9), :, own, :]
+        stage = ST.at[c, 0:count]
+        if leg == 0:
+            pair, to = (src, stage), relay_of(c, up)
+        else:
+            pair, to = (src if ROUTE[c] is None else stage, dst), (middle if up else middle - 1)
+        i = (2 * c + (0 if up else 1)) * 2 + leg
+        return pltpu.make_async_remote_copy(src_ref=pair[0], dst_ref=pair[1], send_sem=hs_.at[i], recv_sem=hr_.at[i],
+                                            device_id=(to, me[1], me[2]), device_id_type=MESH)
+
+    def relay_of(c, up):
+        return ROUTE[c] if up else nx - 1 - ROUTE[c]
+
+    crossings = [(c, up, low_side if up else high_side, high_side if up else low_side) for c in ORDER for up in (True, False)]
+
+    def send_across():
+        for c, up, here, _ in crossings:
+            pl.when(here)(hop(c, up, 1 if ROUTE[c] is None else 0).start)
+
+    def send_planes():
+        for step, c in wide:
+            pl.when(plain(step))(c.start)
+
+    def relay_planes():
+        for c, up, _, _ in crossings:
+            if ROUTE[c] is not None:
+                def forward(c=c, up=up):
+                    hop(c, up, 0).wait_recv()
+                    hop(c, up, 1).start()
+                pl.when(me[0] == relay_of(c, up))(forward)
+
+    def arrive_planes():
+        arrive(thin)
+        for step, c in wide:
+            pl.when(plain(back(step)))(c.wait_recv)
+        for c, up, _, there in crossings:
+            pl.when(there)(hop(c, up, 1).wait_recv)
+
+    def left_planes():
+        left(thin)
+        for step, c in wide:
+            pl.when(plain(step))(c.wait_send)
+        for c, up, here, _ in crossings:
+            if ROUTE[c] is None:
+                pl.when(here)(hop(c, up, 1).wait_send)
+            else:
+                pl.when(here)(hop(c, up, 0).wait_send)
+                pl.when(me[0] == relay_of(c, up))(hop(c, up, 1).wait_send)
 
     def along(copies):
         return [c for c in copies if c[0][0] == 0], [c for c in copies if c[0][0] != 0]
@@ -185,15 +258,24 @@
         for dy in (-1, 0, 1):
             full = TS[k, 0] if plane == 1 and dy == 0 else TR[k, plane, dy + 1]
             if with_x:
-                full = jnp.where(lane % 32 < 4, spread(LR[k, plane, 1, dy + 1], 0), full)
-                full = jnp.where(lane % 32 >= 20, spread(LR[k, plane, 0, dy + 1], 5), full)
+                for side, i, x in ((0, 0, 0), (0, 1, 1), (1, 0, 6), (1, 1, 7)):
+                    here = jnp.logical_and(lane % 32 >= 4 * x, lane % 32 < 4 * x + 4)
+                    full = jnp.where(here, spread(LR[plane, side, dy + 1, i], x), full)
+                far = spread(LR[plane, 1, dy + 1, 2], 0)
+
+            def unfold(shift):
+                part = pltpu.roll(full, shift, 1) if shift else full
+                if with_x:
+                    part = jnp.where(jnp.logical_and(lane >= 32, lane < 36), pltpu.roll(far, (shift + 32) % 128, 1), part)
+                return part
+
             if dy == 0:
                 for g in range(4):
-                    PL[plane, 8 + 8 * g : 16 + 8 * g, :] = pltpu.roll(full, (128 - 32 * g) % 128, 1) if g else full
+                    PL[plane, 8 + 8 * g : 16 + 8 * g, :] = unfold((128 - 32 * g) % 128)
             elif dy == 1:
-                PL[plane, 0:8, :] = pltpu.roll(full, 32, 1)
+                PL[plane, 0:8, :] = unfold(32)
             else:
-                PL[plane, 40:48, :] = full
+                PL[plane, 40:48, :] = unfold(0)
 
     def sweep_z(ref, xs):
         def body(g, carry):
@@ -272,7 +354,7 @@
 
     def from_low(w0, w1, packed, x):
         r0, r1 = pltpu.roll(w0, 1, 1), pltpu.roll(w1, 1, 1)
-        edge = pltpu.roll(packed, 128 - 4 * x, 1) if x else packed
+        edge = pltpu.roll(packed, 132 - 4 * x, 1) if x > 1 else packed
         return jnp.where(first_lane, edge, r0), jnp.where(first_lane, r0, r1)
 
     def forces(xs, finish):
@@ -289,9 +371,9 @@
                     out.append(({i: r0[i] + r1[i] for i in S_Y}, {i: r1[i] - r0[i] for i in D_Y}))
                 return out
 
-            low = sums(xs[0])
+            low = sums(xs[0] - 1)
             for x in xs:
-                high = sums(x + 1)
+                high = sums(x)
                 p0, p1 = x_parts(low[0], high[0]), x_parts(low[1], high[1])
                 for c in range(3):
                     (u0, c0), (u1, c1) = p0[c], p1[c]
@@ -302,39 +384,33 @@
             return carry
         lax.fori_loop(0, 4, body, 0)
 
-    def send_tiles(k, ref, comps, copies):
-        TS[k, 0] = pack(ref, comps, False, range(1, 5))
-        TS[k, 1] = pack(ref, comps, True, range(1, 5))
-        start(copies)
-
-    def put_lines(k, low, high):
-        for z, t in enumerate((low, high)):
-            LS[k, z, 0] = line(t, 1)
-            LS[k, z, 1] = line(t, 4)
-
-    TS[0, 0] = pack(U, 4, False, range(1, 5))
-    TS[0, 1] = pack(U, 4, True, range(1, 5))
-    put_lines(0, TS[0, 0], TS[0, 1])
+    TS[0, 0] = pack(U, 4, False, range(2, 6))
+    TS[0, 1] = pack(U, 4, True, range(2, 6))
+    for z in range(2):
+        for x in range(4):
+            LS[z, x] = line(TS[0, z], x + 2)
 
     t1 = tiles(0, TILES, t1s, t1r)
-    l1 = lines(0, LINES, l1s, l1r)
-    f1, x1 = along(sides(U, SIDES, lambda dx, dy: 4 if dx >= 0 and dy >= 0 else 3, f1s, f1r))
+    l1 = lines(LINES, l1s, l1r)
+    f1, x1 = along(sides(U, [d for d in SIDES if d[1]], 4, slice(2, 6), f1s, f1r))
     t2 = tiles(1, TILES, t2s, t2r)
-    l2 = lines(1, LINES, l2s, l2r)
-    f2, x2 = along(sides(FI, SIDES, lambda dx, dy: 3, f2s, f2r))
+    f2 = sides(FI, [(0, 1), (0, -1)], 3, slice(1, 8), f2s, f2r)
     t3 = tiles(2, LAST_TILES, t3s, t3r)
-    l3 = lines(2, LAST_LINES, l3s, l3r)
-    f3, x3 = along(sides(AD, LAST_SIDES, lambda dx, dy: 3, f3s, f3r))
+    f3 = sides(AD, [(0, -1)], 3, slice(2, 7), f3s, f3r)
 
     block = 1
     for i, n in zip(me, sizes):
         block = block * (1 + (i > 0).astype(jnp.int32) + (i < n - 1).astype(jnp.int32))
     pl.semaphore_wait(barrier, block - 1 + len(rings))
 
+    send_across()
     start(l1)
     start(x1)
     start(t1)
     start(f1)
+    start(thin)
+    send_planes()
+    relay_planes()
 
     def power(xs, total):
         def body(g, total):
@@ -351,13 +427,13 @@
                     q, vm, w, r = load_terms(e, jnp.maximum(U[3, x, lt, rows, :], 0.0))
                     for i in range(6):
                         R6[i, x, lt, rows, :] = r[i]
-                    if x > 0:
+                    if 2 <= x < 6:
                         v2 = vm * vm
                         total = total + jnp.where(inside, v2 * v2, 0.0)
                         tr = (LAM / 16.0) * (e[0] + e[1] + e[2])
                         for i in range(6):
-                            S0[i, x - 1, lt, own, :] = tr + (MU / 8.0) * e[i] if i < 3 else (MU / 16.0) * e[i]
-                        SE[x - 1, lt, own, :] = jnp.where(MT[x - 1, lt, own, :] == 1, (0.5 * BOOST) * (w * q), 0.0)
+                            S0[i, x - 2, lt, own, :] = tr + (MU / 8.0) * e[i] if i < 3 else (MU / 16.0) * e[i]
+                        SE[x - 2, lt, own, :] = jnp.where(MT[x - 2, lt, own, :] == 1, (0.5 * BOOST) * (w * q), 0.0)
             return total
         return lax.fori_loop(0, 5, body, total)
 
@@ -383,77 +459,73 @@
             def sums(x):
                 return [KF[x, lt, pl.ds(base, 8), :] + KF[x, lt, pl.ds(base - 1, 8), :] for lt in range(2)]
 
-            low = sums(xs[0])
+            low = sums(xs[0] - 1)
             for x in xs:
-                high = sums(x + 1)
+                high = sums(x)
                 k0, k1 = low[0] + high[0], low[1] + high[1]
                 s0, s1 = from_low(k0, k1, packed, x)
                 for lt, k in ((0, k0 + s0), (1, k1 + s1)):
-                    fixed = FX[x, lt, own, :].astype(F32)
+                    fixed = U[4, x, lt, pl.ds(base, 8), :]
                     FD[x, lt, own, :] = (1.0 - fixed) / (DIAG * k + fixed)
                 low = high
             return carry
         lax.fori_loop(0, 4, body, 0)
 
     def first_out(c, x, lt, base, own, value):
-        FI[c, x + 1, lt, pl.ds(base, 8), :] = value * FD[x, lt, own, :]
+        FI[c, x, lt, pl.ds(base, 8), :] = value * FD[x, lt, own, :]
+
+    def ring(stage):
+        buf = SUM if stage == 0 else SUM2
+        return [pltpu.make_async_remote_copy(
+            src_ref=buf.at[place[stage]], dst_ref=buf.at[place[stage]],
+            send_sem=ass.at[i], recv_sem=asr.at[i], device_id=peer, device_id_type=MESH)
+            for i, (a, peer) in enumerate(rings) if a == stage]
+
+    def send_sum(stage, value):
+        (SUM if stage == 0 else SUM2)[place[stage]] = value
+        for c in ring(stage):
+            c.start()
+
+    def take_sum(stage):
+        for c in ring(stage):
+            c.wait_recv()
+        buf, n = (SUM, nz) if stage == 0 else (SUM2, nx * ny)
+        value = buf[0]
+        for i in range(1, n):
+            value = value + buf[i]
+        return value
 
     arrive(t1)
     arrive(f1)
     for plane in range(3):
         merge(0, plane, False)
     packed_load()
-    sweep_z(U, range(1, 5))
-    total = power((1, 2, 3), jnp.zeros((8, 128), F32))
-    fill_stiffness(range(1, 5))
-    diagonal((1, 2, 3))
-    forces((1, 2), first_out)
+    sweep_z(U, range(2, 6))
+    total = power((2, 3, 4), jnp.zeros((8, 128), F32))
+    fill_stiffness(range(2, 6))
+    diagonal((3, 4, 5))
+    forces((3, 4), first_out)
 
     arrive(l1)
     arrive(x1)
     for plane in range(3):
         merge(0, plane, True)
     packed_load()
-    sweep_z(U, (0, 5))
-    fill_stiffness((0,))
-    diagonal((0,))
-    power((0,), total)
-    total = power((4,), total)
-    forces((0,), first_out)
-    forces((3,), first_out)
-    start(x2)
-    TS[1, 0] = pack(FI, 3, False, range(1, 5))
-    TS[1, 1] = pack(FI, 3, True, range(1, 5))
-    put_lines(1, TS[1, 0], TS[1, 1])
-    start(l2)
+    arrive_planes()
+    sweep_z(U, (0, 1, 6, 7, 8))
+    fill_stiffness((0, 1, 6, 7))
+    diagonal((1, 2))
+    diagonal((6, 7))
+    total = power((5, 6, 7), total)
+    send_sum(0, jnp.sum(total, axis=0, keepdims=True))
+    power((0, 1), total)
+    forces((1, 2), first_out)
+    forces((5, 6, 7), first_out)
+    start(f2)
+    TS[1, 0] = pack(FI, 3, False, range(1, 8))
+    TS[1, 1] = pack(FI, 3, True, range(1, 8))
     start(t2)
-    start(f2)
-
-    order = (2, 1, 0)
-
-    def ring(stage):
-        axis, out = order[stage], []
-        for i, (a, k, peer) in enumerate(rings):
-            if a == axis:
-                out.append(pltpu.make_async_remote_copy(
-                    src_ref=SUM.at[stage, me[axis]], dst_ref=SUM.at[stage, me[axis]],
-                    send_sem=ass.at[i], recv_sem=asr.at[i], device_id=peer, device_id_type=MESH))
-        return out
-
-    def send_sum(stage, value):
-        SUM[stage, me[order[stage]]] = value
-        for c in ring(stage):
-            c.start()
-
-    def take_sum(stage):
-        for c in ring(stage):
-            c.wait_recv()
-        value = SUM[stage, 0]
-        for i in range(1, sizes[order[stage]]):
-            value = value + SUM[stage, i]
-        return value
-
-    send_sum(0, total)
+    send_sum(1, take_sum(0))
 
     def stiff(xs):
         def body(g, carry):
@@ -474,9 +546,10 @@
         packed_forces(stiff_terms(packed_strain(), kp_ref[...]))
 
     def adjoint_out(c, x, lt, base, own, value):
-        new = (1.0 + RELAX) * FI[c, x + 1, lt, pl.ds(base, 8), :] - RELAX * FD[x, lt, own, :] * value
-        AD[c, x + 1, lt, pl.ds(base, 8), :] = new
-        adj_out[c, x, lt, own, :] = new
+        new = (1.0 + RELAX) * FI[c, x, lt, pl.ds(base, 8), :] - RELAX * FD[x, lt, own, :] * value
+        AD[c, x, lt, pl.ds(base, 8), :] = new
+        if x < 6:
+            adj_out[c, x - 2, lt, own, :] = new
 
     kp_ref = PK.at[6, 0:40]
     arrive(t2)
@@ -484,28 +557,12 @@
     for plane in range(3):
         merge(1, plane, False)
     packed_stiff()
-    sweep_z(FI, range(1, 5))
-    stiff((1, 2, 3))
-    forces((1, 2), adjoint_out)
-    send_sum(1, take_sum(0))
-    arrive(l2)
-    arrive(x2)
-    for plane in range(3):
-        merge(1, plane, True)
-    packed_stiff()
-    sweep_z(FI, (0, 5))
-    stiff((0,))
-    forces((0,), adjoint_out)
-    start(x3)
-    edge = pack(AD, 3, False, (1,))
-    LS[2, 0, 0] = line(edge, 1)
-    start(l3)
-    stiff((4,))
-    forces((3,), adjoint_out)
-    TS[2, 0] = edge + pack(AD, 3, False, (2, 3, 4))
+    sweep_z(FI, range(1, 8))
+    stiff(range(1, 7))
+    forces(range(2, 7), adjoint_out)
+    start(f3)
+    TS[2, 0] = pack(AD, 3, False, range(2, 7))
     start(t3)
-    start(f3)
-    send_sum(2, take_sum(1))
 
     def last(xs):
         def body(g, carry):
@@ -513,15 +570,15 @@
             rows = pl.ds(base, 8)
             own = pl.ds(pl.multiple_of(8 * g, 8), 8)
             for lt in range(2):
-                low = y_sums(xs[0] + 1, lt, base)
+                low = y_sums(xs[0] + 2, lt, base)
                 for x in xs:
-                    high = y_sums(x + 2, lt, base)
+                    high = y_sums(x + 3, lt, base)
                     e = strain6(gradients(low, high))
                     low = high
                     dot = e[0] * S0[0, x, lt, own, :]
                     for i in range(1, 6):
                         dot = dot + e[i] * S0[i, x, lt, own, :]
-                    d = U[3, x + 1, lt, rows, :]
+                    d = U[3, x + 2, lt, rows, :]
                     slope = jnp.where(MT[x, lt, own, :] == 1, 3.0 * (d * d), 0.0)
                     sens_out[x, lt, own, :] = SE[x, lt, own, :] - slope * dot
             return carry
@@ -530,17 +587,13 @@
     arrive(t3)
     arrive(f3)
     merge(2, 2, False)
-    sweep_z(AD, range(1, 5))
-    last((0, 1, 2))
-    arrive(l3)
-    arrive(x3)
-    merge(2, 2, True)
-    sweep_z(AD, (5,))
-    last((3,))
-    sum_out[...] = take_sum(2)
-    for copies in (t1, l1, f1, x1, t2, l2, f2, x2, t3, l3, f3, x3):
+    sweep_z(AD, range(2, 7))
+    last((0, 1, 2, 3))
+    sum_out[...] = take_sum(1)
+    left_planes()
+    for copies in (t1, l1, f1, x1, t2, f2, t3, f3):
         left(copies)
-    for stage in range(3):
+    for stage in range(2):
         for c in ring(stage):
             c.wait_send()
 
@@ -558,7 +611,7 @@
 
 def solution(mesh):
     sizes = tuple(mesh.shape[a] for a in ("gx", "gy", "gz"))
-    peers = sum(sizes) - 3
+    peers = sizes[2] - 1 + sizes[0] * sizes[1] - 1
     count = sizes[0] * sizes[1] * sizes[2] * 4 * 32 * 256
 
     def per_device(displacement, density, material, fixed_mask):
@@ -568,35 +621,36 @@
         adj, sens, total = pl.pallas_call(
             functools.partial(kernel, sizes),
             out_shape=(jax.ShapeDtypeStruct((3, 4, 2, 32, 128), F32), jax.ShapeDtypeStruct((4, 2, 32, 128), F32),
-                       jax.ShapeDtypeStruct((8, 128), F32)),
+                       jax.ShapeDtypeStruct((1, 128), F32)),
             in_specs=[pl.BlockSpec(memory_space=pl.ANY)] * 4,
             out_specs=[vmem] * 3,
             scratch_shapes=[
-                pltpu.VMEM((4, 6, 2, ROWS, 128), F32),
-                pltpu.VMEM((3, 6, 2, ROWS, 128), F32),
-                pltpu.VMEM((3, 6, 2, ROWS, 128), F32),
+                pltpu.VMEM((5, 9, 2, ROWS, 128), F32),
+                pltpu.VMEM((3, 9, 2, ROWS, 128), F32),
+                pltpu.VMEM((3, 9, 2, ROWS, 128), F32),
                 pltpu.VMEM((4, 2, 32, 128), F32),
                 pltpu.VMEM((4, 2, 32, 128), jnp.int32),
                 pltpu.VMEM((4, 2, 32, 128), jnp.int32),
-                pltpu.VMEM((3, 6, 2, ROWS, 128), F32),
-                pltpu.VMEM((3, 6, 2, ROWS, 128), F32),
-                pltpu.VMEM((6, 5, 2, ROWS, 128), F32),
-                pltpu.VMEM((5, 2, ROWS, 128), F32),
+                pltpu.VMEM((3, 9, 2, ROWS, 128), F32),
+                pltpu.VMEM((3, 9, 2, ROWS, 128), F32),
+                pltpu.VMEM((6, 8, 2, ROWS, 128), F32),
+                pltpu.VMEM((8, 2, ROWS, 128), F32),
                 pltpu.VMEM((6, 4, 2, 32, 128), F32),
                 pltpu.VMEM((4, 2, 32, 128), F32),
-                pltpu.VMEM((4, 2, 32, 128), F32),
+                pltpu.VMEM((8, 2, 32, 128), F32),
                 pltpu.VMEM((3, 2, 8, 128), F32),
-                pltpu.VMEM((3, 2, 2, 1, 128), F32),
+                pltpu.VMEM((2, 4, 1, 128), F32),
                 pltpu.VMEM((3, 3, 3, 8, 128), F32),
-                pltpu.VMEM((3, 3, 2, 3, 1, 128), F32),
+                pltpu.VMEM((3, 2, 3, 3, 1, 128), F32),
                 pltpu.VMEM((3, ROWS, 128), F32),
                 pltpu.VMEM((7, ROWS, 128), F32),
                 pltpu.VMEM((4, 32, 128), F32),
-                pltpu.VMEM((3, 8, 8, 128), F32),
+                pltpu.VMEM((sizes[2], 1, 128), F32),
+                pltpu.VMEM((sizes[0] * sizes[1], 1, 128), F32),
+                pltpu.VMEM((3, 3, 2, 32, 128), F32),
                 dma((8,)),
-                *both(8), *both(8), *both(18),
-                *both(8), *both(8), *both(18),
-                *both(3), *both(2), *both(2),
+                *both(4), *both(12), *both(6), *both(8), *both(18),
+                *both(2), *both(8), *both(1), *both(2),
                 *both(peers),
             ],
             compiler_params=pltpu.CompilerParams(collective_id=0, has_side_effects=True),

time: 44.9 us -> 42.7 us (0.951)
  Pallas kernels: 44 us -> 42 us
    pallas_call x1, Pallas kernels: 42 us -> 39.9 us  [per_device(): pl.pallas_call(functools.partial(kernel, sizes), out_shape=(jax.ShapeDtyp...]
where the time goes in v3:
time: 42.7 us; the launch traced here: 42.6 us
  Pallas kernels  42 us (98%)
  between operations  0.64 us (1%)
    pallas_call x1, Pallas kernels, per_device(): pl.pallas_call(functools.partial(kernel, sizes), out_shape=(jax.ShapeDtyp...  39.9 us
    pallas_call x1, Pallas kernels, per_device(): pl.pallas_call(functools.partial(finish_kernel, count), out_shape=(jax.Sh...  2.03 us

profile of v3, /device:TPU:1, one launch (start us, length us, event | category | flops | bytes accessed | tf_op | source)
XLA Modules:
  0.0 42.6 jit_solution(9478487742373203243)
XLA Ops:
  0.6 39.9 %shard_map.59 = (f32[3,4,2,32,128]{4,3,2,1,0:T(8,128)}, f32[4,2,32,128]{3,2,1,0:T(8,128)}, f32[1,128]{1,0:T(1,128)}) custom-call(f32[3,4,32,256]{3,2,1,0:T(8,128)} %disp.1, f32[4,32,256]{2,1,0:T(8,128)} %dens.1, s32[4,32,256]{2,1,0:T(8,128)} %mat.1, s32[4,32,256]{2,1,0:T(8,128)} %fix.1), custom_call_target="tpu_custom_call" | custom-call | tf_op jit(solution)/shard_map/pallas_call | solution.py:621
  40.6 2.0 %shard_map.60 = (f32[3,4,32,256]{3,2,1,0:T(8,128)}, f32[4,32,256]{2,1,0:T(8,128)}) custom-call(f32[3,4,2,32,128]{4,3,2,1,0:T(8,128)} %get-tuple-element.5.adj, f32[4,2,32,128]{3,2,1,0:T(8,128)} %get-tuple-element.6.sens, f32[1,128]{1,0:T(1,128)} %get-tuple-element.7.total), custom_call_target="tpu_custom_call" | custom-call | tf_op jit(solution)/shard_map/pallas_call | solution.py:658

commit v4 on v3

--- a/solution.py
+++ b/solution.py
@@ -620,8 +620,7 @@
         both = lambda n: [dma((n,)), dma((n,))]
         adj, sens, total = pl.pallas_call(
             functools.partial(kernel, sizes),
-            out_shape=(jax.ShapeDtypeStruct((3, 4, 2, 32, 128), F32), jax.ShapeDtypeStruct((4, 2, 32, 128), F32),
-                       jax.ShapeDtypeStruct((1, 128), F32)),
+            out_shape=(pltpu.VMEM((3, 4, 2, 32, 128), F32), pltpu.VMEM((4, 2, 32, 128), F32), pltpu.VMEM((1, 128), F32)),
             in_specs=[pl.BlockSpec(memory_space=pl.ANY)] * 4,
             out_specs=[vmem] * 3,
             scratch_shapes=[
@@ -660,7 +659,7 @@
             out_shape=(jax.ShapeDtypeStruct((3, 4, 32, 256), F32), jax.ShapeDtypeStruct((4, 32, 256), F32)),
             in_specs=[vmem] * 3,
             out_specs=[vmem] * 2,
-        )(adj, sens, total)
+        )(*(pltpu.with_memory_space_constraint(v, pltpu.VMEM) for v in (adj, sens, total)))
 
     placed = (P(None, "gx", "gy", "gz"), P("gx", "gy", "gz"), P("gx", "gy", "gz"), P("gx", "gy", "gz"))
     return jax.shard_map(per_device, mesh=mesh, in_specs=placed, out_specs=(placed[0], placed[1]), check_vma=False)

time: 42.7 us -> 40.9 us (0.958)
  Pallas kernels: 42 us -> 40.1 us
    pallas_call x1, Pallas kernels: 2.03 us -> 0.97 us  [per_device(): pl.pallas_call(functools.partial(finish_kernel, count), out_shape=(jax.Sh...]
    pallas_call x1, Pallas kernels: 39.9 us -> 39.2 us  [per_device(): pl.pallas_call(functools.partial(kernel, sizes), out_shape=(pltpu.VMEM((3...]
where the time goes in v4:
time: 40.9 us; the launch traced here: 40.8 us
  Pallas kernels  40.1 us (98%)
  between operations  0.64 us (2%)
    pallas_call x1, Pallas kernels, per_device(): pl.pallas_call(functools.partial(kernel, sizes), out_shape=(pltpu.VMEM((3...  39.2 us
    pallas_call x1, Pallas kernels, per_device(): pl.pallas_call(functools.partial(finish_kernel, count), out_shape=(jax.Sh...  0.97 us

profile of v4, /device:TPU:1, one launch (start us, length us, event | category | flops | bytes accessed | tf_op | source)
XLA Modules:
  0.0 40.8 jit_solution(7578576759333253709)
XLA Ops:
  0.6 39.2 %shard_map.59 = (f32[3,4,2,32,128]{4,3,2,1,0:T(8,128)S(1)}, f32[4,2,32,128]{3,2,1,0:T(8,128)S(1)}, f32[1,128]{1,0:T(1,128)S(1)}) custom-call(f32[3,4,32,256]{3,2,1,0:T(8,128)} %disp.1, f32[4,32,256]{2,1,0:T(8,128)} %dens.1, s32[4,32,256]{2,1,0:T(8,128)} %mat.1, s32[4,32,256]{2,1,0:T(8,128)} %fix.1), custom_call_target="tpu_custom_call" | custom-call | tf_op jit(solution)/shard_map/pallas_call | solution.py:621
  39.8 1.0 %shard_map.60 = (f32[3,4,32,256]{3,2,1,0:T(8,128)}, f32[4,32,256]{2,1,0:T(8,128)}) custom-call(f32[3,4,2,32,128]{4,3,2,1,0:T(8,128)S(1)} %get-tuple-element.5.adj, f32[4,2,32,128]{3,2,1,0:T(8,128)S(1)} %get-tuple-element.6.sens, f32[1,128]{1,0:T(1,128)S(1)} %get-tuple-element.7.total), custom_call_target="tpu_custom_call" | custom-call | tf_op jit(solution)/shard_map/pallas_call | solution.py:657

commit v5 on v4

--- a/solution.py
+++ b/solution.py
@@ -222,7 +222,6 @@
                 pl.when(me[0] == relay_of(c, up))(forward)
 
     def arrive_planes():
-        arrive(thin)
         for step, c in wide:
             pl.when(plain(back(step)))(c.wait_recv)
         for c, up, _, there in crossings:
@@ -277,22 +276,25 @@
             else:
                 PL[plane, 40:48, :] = unfold(0)
 
-    def sweep_z(ref, xs):
+    def sweep_z(ref, xs, lts=(0, 1), begin=7, count=5, stride=8):
         def body(g, carry):
-            rows = pl.ds(7 + 8 * g, 8)
-            edge = PL[2, rows, :]
+            rows = pl.ds(begin + stride * g, 8)
+            edge = PL[2, rows, :] if 1 in lts else None
             for c in range(3):
                 for x in xs:
-                    t0, t1 = ref[c, x, 0, rows, :], ref[c, x, 1, rows, :]
-                    r0, r1 = pltpu.roll(t0, 127, 1), pltpu.roll(t1, 127, 1)
-                    s0 = jnp.where(last_lane, r1, r0)
-                    s1 = jnp.where(last_lane, pltpu.roll(edge, 127 - 4 * x - c, 1), r1)
-                    PS[c, x, 0, rows, :] = s0 + t0
-                    PS[c, x, 1, rows, :] = s1 + t1
-                    QS[c, x, 0, rows, :] = s0 - t0
-                    QS[c, x, 1, rows, :] = s1 - t1
+                    t1 = ref[c, x, 1, rows, :]
+                    r1 = pltpu.roll(t1, 127, 1)
+                    if 0 in lts:
+                        t0 = ref[c, x, 0, rows, :]
+                        s0 = jnp.where(last_lane, r1, pltpu.roll(t0, 127, 1))
+                        PS[c, x, 0, rows, :] = s0 + t0
+                        QS[c, x, 0, rows, :] = s0 - t0
+                    if 1 in lts:
+                        s1 = jnp.where(last_lane, pltpu.roll(edge, 127 - 4 * x - c, 1), r1)
+                        PS[c, x, 1, rows, :] = s1 + t1
+                        QS[c, x, 1, rows, :] = s1 - t1
             return carry
-        lax.fori_loop(0, 5, body, 0)
+        lax.fori_loop(0, count, body, 0)
 
     def gradients(low, high):
         return [[high[c][0] - low[c][0] for c in range(3)], [high[c][1] + low[c][1] for c in range(3)],
@@ -511,11 +513,12 @@
     for plane in range(3):
         merge(0, plane, True)
     packed_load()
-    arrive_planes()
-    sweep_z(U, (0, 1, 6, 7, 8))
+    arrive(thin)
     fill_stiffness((0, 1, 6, 7))
     diagonal((1, 2))
     diagonal((6, 7))
+    arrive_planes()
+    sweep_z(U, (0, 1, 6, 7, 8))
     total = power((5, 6, 7), total)
     send_sum(0, jnp.sum(total, axis=0, keepdims=True))
     power((0, 1), total)
@@ -525,13 +528,12 @@
     TS[1, 0] = pack(FI, 3, False, range(1, 8))
     TS[1, 1] = pack(FI, 3, True, range(1, 8))
     start(t2)
-    send_sum(1, take_sum(0))
-
-    def stiff(xs):
+
+    def stiff(xs, lts, begin, count, stride):
         def body(g, carry):
-            base = pl.multiple_of(8 * g, 8)
+            base = pl.multiple_of(begin + stride * g, 8)
             rows = pl.ds(base, 8)
-            for lt in range(2):
+            for lt in lts:
                 low = y_sums(xs[0], lt, base)
                 for x in xs:
                     high = y_sums(x + 1, lt, base)
@@ -540,7 +542,7 @@
                     for i in range(6):
                         R6[i, x, lt, rows, :] = r[i]
             return carry
-        lax.fori_loop(0, 5, body, 0)
+        lax.fori_loop(0, count, body, 0)
 
     def packed_stiff():
         packed_forces(stiff_terms(packed_strain(), kp_ref[...]))
@@ -552,24 +554,29 @@
             adj_out[c, x - 2, lt, own, :] = new
 
     kp_ref = PK.at[6, 0:40]
+    sweep_z(FI, range(1, 8), (0,), 8, 4)
+    stiff(range(1, 7), (0,), 8, 3, 8)
+    send_sum(1, take_sum(0))
     arrive(t2)
     arrive(f2)
     for plane in range(3):
         merge(1, plane, False)
     packed_stiff()
-    sweep_z(FI, range(1, 8))
-    stiff(range(1, 7))
+    sweep_z(FI, range(1, 8), (1,))
+    sweep_z(FI, range(1, 8), (0,), 0, 2, 40)
+    stiff(range(1, 7), (0,), 0, 2, 32)
+    stiff(range(1, 7), (1,), 0, 5, 8)
     forces(range(2, 7), adjoint_out)
     start(f3)
     TS[2, 0] = pack(AD, 3, False, range(2, 7))
     start(t3)
 
-    def last(xs):
+    def last(xs, lts, begin, count):
         def body(g, carry):
-            base = pl.multiple_of(8 + 8 * g, 8)
+            base = pl.multiple_of(begin + 8 * g, 8)
             rows = pl.ds(base, 8)
-            own = pl.ds(pl.multiple_of(8 * g, 8), 8)
-            for lt in range(2):
+            own = pl.ds(pl.multiple_of(begin - 8 + 8 * g, 8), 8)
+            for lt in lts:
                 low = y_sums(xs[0] + 2, lt, base)
                 for x in xs:
                     high = y_sums(x + 3, lt, base)
@@ -582,13 +589,17 @@
                     slope = jnp.where(MT[x, lt, own, :] == 1, 3.0 * (d * d), 0.0)
                     sens_out[x, lt, own, :] = SE[x, lt, own, :] - slope * dot
             return carry
-        lax.fori_loop(0, 4, body, 0)
-
+        lax.fori_loop(0, count, body, 0)
+
+    sweep_z(AD, range(2, 7), (0,), 8, 4)
+    last((0, 1, 2, 3), (0,), 8, 3)
     arrive(t3)
     arrive(f3)
     merge(2, 2, False)
-    sweep_z(AD, range(2, 7))
-    last((0, 1, 2, 3))
+    sweep_z(AD, range(2, 7), (1,))
+    sweep_z(AD, range(2, 7), (0,), 40, 1)
+    last((0, 1, 2, 3), (0,), 32, 1)
+    last((0, 1, 2, 3), (1,), 8, 4)
     sum_out[...] = take_sum(1)
     left_planes()
     for copies in (t1, l1, f1, x1, t2, f2, t3, f3):

time: 40.9 us -> 40.1 us (0.980)
  Pallas kernels: 40.1 us -> 39.4 us
    pallas_call x1, Pallas kernels: 39.2 us -> 38.4 us  [per_device(): pl.pallas_call(functools.partial(kernel, sizes), out_shape=(pltpu.VMEM((3...]
where the time goes in v5:
time: 40.1 us; the launch traced here: 40 us
  Pallas kernels  39.4 us (98%)
  between operations  0.64 us (2%)
    pallas_call x1, Pallas kernels, per_device(): pl.pallas_call(functools.partial(kernel, sizes), out_shape=(pltpu.VMEM((3...  38.4 us
    pallas_call x1, Pallas kernels, per_device(): pl.pallas_call(functools.partial(finish_kernel, count), out_shape=(jax.Sh...  0.97 us

profile of v5, /device:TPU:1, one launch (start us, length us, event | category | flops | bytes accessed | tf_op | source)
XLA Modules:
  0.0 40.0 jit_solution(6011995868954099036)
XLA Ops:
  0.6 38.4 %shard_map.59 = (f32[3,4,2,32,128]{4,3,2,1,0:T(8,128)S(1)}, f32[4,2,32,128]{3,2,1,0:T(8,128)S(1)}, f32[1,128]{1,0:T(1,128)S(1)}) custom-call(f32[3,4,32,256]{3,2,1,0:T(8,128)} %disp.1, f32[4,32,256]{2,1,0:T(8,128)} %dens.1, s32[4,32,256]{2,1,0:T(8,128)} %mat.1, s32[4,32,256]{2,1,0:T(8,128)} %fix.1), custom_call_target="tpu_custom_call" | custom-call | tf_op jit(solution)/shard_map/pallas_call | solution.py:632
  39.0 1.0 %shard_map.60 = (f32[3,4,32,256]{3,2,1,0:T(8,128)}, f32[4,32,256]{2,1,0:T(8,128)}) custom-call(f32[3,4,2,32,128]{4,3,2,1,0:T(8,128)S(1)} %get-tuple-element.5.adj, f32[4,2,32,128]{3,2,1,0:T(8,128)S(1)} %get-tuple-element.6.sens, f32[1,128]{1,0:T(1,128)S(1)} %get-tuple-element.7.total), custom_call_target="tpu_custom_call" | custom-call | tf_op jit(solution)/shard_map/pallas_call | solution.py:668

commit v6 on v5

--- a/solution.py
+++ b/solution.py
@@ -406,11 +406,11 @@
     pl.semaphore_wait(barrier, block - 1 + len(rings))
 
     send_across()
+    start(thin)
+    start(x1)
     start(l1)
-    start(x1)
     start(t1)
     start(f1)
-    start(thin)
     send_planes()
     relay_planes()
 

time: 40.1 us -> 40 us (level)
  no operation moved by 1% of the time
where the time goes in v6:
time: 40 us; the launch traced here: 39.9 us
  Pallas kernels  39.2 us (98%)
  between operations  0.64 us (2%)
    pallas_call x1, Pallas kernels, per_device(): pl.pallas_call(functools.partial(kernel, sizes), out_shape=(pltpu.VMEM((3...  38.3 us
    pallas_call x1, Pallas kernels, per_device(): pl.pallas_call(functools.partial(finish_kernel, count), out_shape=(jax.Sh...  0.97 us

profile of v6, /device:TPU:1, one launch (start us, length us, event | category | flops | bytes accessed | tf_op | source)
XLA Modules:
  0.0 39.9 jit_solution(3405280213458616427)
XLA Ops:
  0.6 38.3 %shard_map.59 = (f32[3,4,2,32,128]{4,3,2,1,0:T(8,128)S(1)}, f32[4,2,32,128]{3,2,1,0:T(8,128)S(1)}, f32[1,128]{1,0:T(1,128)S(1)}) custom-call(f32[3,4,32,256]{3,2,1,0:T(8,128)} %disp.1, f32[4,32,256]{2,1,0:T(8,128)} %dens.1, s32[4,32,256]{2,1,0:T(8,128)} %mat.1, s32[4,32,256]{2,1,0:T(8,128)} %fix.1), custom_call_target="tpu_custom_call" | custom-call | tf_op jit(solution)/shard_map/pallas_call | solution.py:632
  38.9 1.0 %shard_map.60 = (f32[3,4,32,256]{3,2,1,0:T(8,128)}, f32[4,32,256]{2,1,0:T(8,128)}) custom-call(f32[3,4,2,32,128]{4,3,2,1,0:T(8,128)S(1)} %get-tuple-element.5.adj, f32[4,2,32,128]{3,2,1,0:T(8,128)S(1)} %get-tuple-element.6.sens, f32[1,128]{1,0:T(1,128)S(1)} %get-tuple-element.7.total), custom_call_target="tpu_custom_call" | custom-call | tf_op jit(solution)/shard_map/pallas_call | solution.py:668
